TPU v7x, 128 devices: a whole 4x4x4 slice. The times are simulated.
128 devices in a mesh: slab: 4 (over y), brick: 32 (over z, x, core).
Axes of the slice: x: 4, y: 4, z: 4, core: 2. Of those that a mesh axis runs over, the one named last changes fastest.
Arguments:
- verts: float32 [131072, 3, 128], P(('slab', 'brick')), may hold values from -4.2 to 4.2
- stiffness: float32 [131072, 128], P(('slab', 'brick')), may hold values from 0.2 to 2
- local_pairs: int32 [128, 2, 256], P(('slab', 'brick')), may hold values from 0 to 1023, as said below
- border_pick: int32 [128, 128], P(('slab', 'brick')), may hold values from 0 to 1023
- recv_src: int32 [128, 32, 8], P(('slab', 'brick')), may hold values from 0 to 127
- recv_pair: int32 [128, 32, 8], P(('slab', 'brick')), may hold values from -1 to 1023, as said below
- face_pick: int32 [128, 2, 64], P(('slab', 'brick')), may hold values from 0 to 1023
- face_pair: int32 [128, 2, 64], P(('slab', 'brick')), may hold values from -1 to 1023, as said below
Outputs:
- membrane_force: float32 [131072, 3, 128], P(('slab', 'brick'))
Inputs may be any that keep to these rules, and one draw needn't show every extreme that they name: `local_pairs`: the two rows of a pair name different patches. `recv_pair`: -1 marks an empty slot; the slots for a device's own brick are empty. `face_pair`: -1 marks an empty slot.
All inputs are finite; a program needn't handle non-finite values.
Results may differ from a plain program's by a relative error of at most 0.0001.
Values sent between devices are 32-bit elements; how exact they have to be, the bound alone decides.
A program may use at most 128 MiB of HBM per device.

v0:
```python
import math

import jax
import jax.numpy as jnp
from jax import lax
from jax.sharding import PartitionSpec as P

highest = lax.Precision.HIGHEST


def with_halo(cells, sides, width):
    for axis, dim in sides:
        count = lax.axis_size(axis)
        ends = count - 1
        head = lax.slice_in_dim(cells, 0, width, axis=dim)
        tail = lax.slice_in_dim(cells, cells.shape[dim] - width, cells.shape[dim], axis=dim)
        cells = jnp.concatenate(
            [
                lax.ppermute(tail, axis, [(i, (i + 1) % count) for i in range(ends)]),
                cells,
                lax.ppermute(head, axis, [((i + 1) % count, i) for i in range(ends)]),
            ],
            axis=dim,
        )
    return cells


def centroids(points):
    return (points + jnp.roll(points, -1, axis=-1) + jnp.roll(points, -2, axis=-1)) / 3.0


def tile_forces(own_points, far_centres, far_weight):
    own_sq = jnp.sum(own_points * own_points, axis=1)
    far_sq = jnp.sum(far_centres * far_centres, axis=1)
    cross_dot = jnp.einsum("pci,pcj->pij", own_points, far_centres, precision=highest)
    dist_sq = own_sq[:, :, None] + far_sq[:, None, :] - 2.0 * cross_dot
    energy = far_weight[:, None, :] * jnp.exp(-0.5 * dist_sq) / own_points.shape[-1]
    row_total = jnp.sum(energy, axis=2)
    col_total = jnp.sum(energy, axis=1)
    pushed = own_points * row_total[:, None, :] - jnp.einsum(
        "pcj,pij->pci", far_centres, energy, precision=highest
    )
    reaction = far_centres * col_total[:, None, :] - jnp.einsum(
        "pci,pij->pcj", own_points, energy, precision=highest
    )
    return (pushed, reaction)


def blocked(func, arrays):
    count = arrays[0].shape[0]
    step_rows = math.gcd(count, 16)
    shaped = tuple(
        (array.reshape((count // step_rows, step_rows) + array.shape[1:]) for array in arrays)
    )
    results = lax.map(func, shaped)
    return tuple((result.reshape((count,) + result.shape[2:]) for result in results))


def body(verts, stiffness, local_pairs, border_pick, recv_src, recv_pair, face_pick, face_pair):
    vert_count = verts.shape[-1]
    centres = centroids(verts)

    def pack_rows(rows):
        return jnp.concatenate([verts[rows], stiffness[rows][..., None, :]], axis=-2)

    def remote(packed, targets, allowed, pushed):
        usable = (targets >= 0) & allowed
        clipped = jnp.maximum(targets, 0)

        def far_tiles(pieces):
            target_idx, packed_rows, usable_rows = pieces
            weight = packed_rows[:, 3] * usable_rows.astype(jnp.float32)[:, None]
            return tile_forces(verts[target_idx], centroids(packed_rows[:, :3]), weight)

        push_far, react_far = blocked(far_tiles, (clipped, packed, usable))
        return (pushed.at[clipped].add(push_far), react_far)

    target_loc = local_pairs[0, 0]
    anchor_loc = local_pairs[0, 1]

    def local_tiles(pieces):
        target_idx, anchor_idx = pieces
        return tile_forces(verts[target_idx], centres[anchor_idx], stiffness[anchor_idx])

    push_loc, react_loc = blocked(local_tiles, (target_loc, anchor_loc))
    pushed = jnp.zeros_like(verts).at[target_loc].add(push_loc)
    reaction = jnp.zeros_like(verts).at[anchor_loc].add(react_loc)
    brick_pushed = pushed
    brick_reaction = reaction
    bricks = lax.axis_size("brick")
    border_count = border_pick.shape[1]
    every = lax.all_gather(pack_rows(border_pick[0]), "brick", axis=0, tiled=True)
    flat = (jnp.arange(bricks, dtype=jnp.int32)[:, None] * border_count + recv_src[0]).reshape(-1)
    brick_pushed, react_far = remote(every[flat], recv_pair[0].reshape(-1), True, brick_pushed)
    partial_sums = (
        jnp.zeros((bricks * border_count, 3, vert_count), jnp.float32).at[flat].add(react_far)
    )
    mine = lax.psum_scatter(partial_sums, "brick", scatter_dimension=0, tiled=True)
    brick_reaction = brick_reaction.at[border_pick[0]].add(mine)
    pushed = brick_pushed
    face_pushed = pushed
    face_reaction = brick_reaction
    facing = face_pick.shape[2]
    rows = face_pick[0].reshape(-1)
    extended = with_halo(pack_rows(rows), (("slab", 0),), facing)
    incoming = jnp.concatenate([extended[:facing], extended[3 * facing :]], axis=0)
    layer = lax.axis_index("slab")
    layers = lax.axis_size("slab")
    allowed = jnp.concatenate(
        [jnp.full((facing,), layer > 0), jnp.full((facing,), layer < layers - 1)]
    )
    face_pushed, react_far = remote(incoming, face_pair[0].reshape(-1), allowed, face_pushed)
    returned = with_halo(react_far, (("slab", 0),), facing)
    face_reaction = face_reaction.at[rows[:facing]].add(returned[:facing])
    face_reaction = face_reaction.at[rows[facing:]].add(returned[3 * facing :])
    pushed = face_pushed
    return (
        pushed
        + (
            face_reaction
            + jnp.roll(face_reaction, 1, axis=-1)
            + jnp.roll(face_reaction, 2, axis=-1)
        )
        / 3.0
    )


def solution(mesh):
    placed = (
        P(("slab", "brick"), None, None),
        P(("slab", "brick"), None),
        P(("slab", "brick"), None, None),
        P(("slab", "brick"), None),
        P(("slab", "brick"), None, None),
        P(("slab", "brick"), None, None),
        P(("slab", "brick"), None, None),
        P(("slab", "brick"), None, None),
    )
    return jax.shard_map(
        body,
        mesh=mesh,
        in_specs=placed,
        out_specs=P(("slab", "brick"), None, None),
        check_vma=False,
    )
```

profile of v0, /device:TPU:1, one launch (start us, length us, event | category | flops | bytes accessed | tf_op | source)
XLA Modules:
  0.0 614.5 jit_solution(14328518103817302794)
XLA Ops:
  11.9 4.0 collective-permute-start
  20.8 2.5 copy.41
  23.3 2.5 slice.170
  25.9 2.4 slice.168
  28.9 6.1 fusion.52
  36.0 147.4 %while.36 = (s32[]{:T(128)}, f32[16,16,3,128]{3,2,1,0:T(4,128)}, f32[16,16,3,128]{3,2,1,0:T(4,128)S(1)}, s32[16,16]{1,0:T(8,128)S(1)}, f32[1024,3,128]{2,1,0:T(4...) while((s32[]{:T(128)}, f32[16,16,3,128]{3,2,1,0:T(4,128)}, ...), condition=%wide.region_5.6_spmd, body=%wide.region_0.5_spmd.sunk | while | flops 30451808 | bytes 3621553 | solution.py:55
  39.5 2.4 fusion.117
  48.7 2.4 fusion.117
  57.9 2.4 fusion.117
  67.2 2.4 fusion.117
  76.5 2.4 fusion.117
  85.7 2.4 fusion.117
  94.9 2.4 fusion.117
  159.3 2.4 fusion.117
  168.5 2.4 fusion.117
  187.0 8.3 %scatter_fusion = f32[1024,3,128]{2,1,0:T(4,128)S(1)} fusion(f32[1024,3,128]{2,1,0:T(4,128)S(1)} %broadcast.310, s32[256]{0:T(256)S(1)} %bitcast.222, f32[256,3,128]{2,1,0:T(4,128)S(1)} %bitcast.206), kind=kCustom, calls=%fused_computation.10 | custom fusion | flops 98304 | bytes 1180672 | tf_op jit(solution)/shard_map/scatter-add | solution.py:87
  196.3 11.8 %copy.44 = f32[4096,4,128]{2,1,0:T(4,128)} copy(f32[4096,4,128]{2,0,1:T(8,128)} %all-gather.2.cloned.1.call-done) | data formatting | bytes 16777216 | tf_op jit(solution)/shard_map/all_gather | solution.py:92
  208.2 5.1 gather_fusion.7
  214.3 146.0 %while.37 = (s32[]{:T(128)}, f32[16,16,3,128]{3,2,1,0:T(4,128)S(1)}, f32[16,16,3,128]{3,2,1,0:T(4,128)}, s32[16,16]{1,0:T(8,128)S(1)}, f32[1024,3,128]{2,1,0:T(4...) while((s32[]{:T(128)}, f32[16,16,3,128]{3,2,1,0:T(4,128)S(1)}, ...), condition=%wide.region_12.13_spmd, body=%wide.region_7.0_spmd.sunk | while | flops 30497856 | bytes 3820929 | solution.py:55
  360.3 3.9 broadcast_in_dim.42
  364.2 24.9 %scatter_fusion.1 = f32[4096,3,128]{2,1,0:T(4,128)} fusion(f32[4096,3,128]{2,1,0:T(4,128)} %broadcast_in_dim.42, s32[256]{0:T(256)S(1)} %bitcast.220, f32[256,3,128]{2,1,0:T(4,128)S(1)} %bitcast.209), kind=kCustom, calls=%fused_computation.11 | custom fusion | flops 98304 | bytes 1180672 | tf_op jit(solution)/shard_map/scatter-add | solution.py:96
  390.1 67.5 %while.38 = (s32[]{:T(128)}, f32[8,16,3,128]{3,2,1,0:T(4,128)}, f32[8,16,3,128]{3,2,1,0:T(4,128)S(1)}, s32[8,16]{1,0:T(8,128)S(1)}, f32[1024,3,128]{2,1,0:T(4,12...) while((s32[]{:T(128)}, f32[8,16,3,128]{3,2,1,0:T(4,128)}, ...), condition=%wide.region_21.22_spmd, body=%wide.region_16.21_spmd.sunk | while | flops 30497856 | bytes 3886465 | solution.py:55
  457.6 3.9 collective-permute-start.2
  462.8 51.9 %all-reduce.4.cloned.1.call-done = f32[4096,3,128]{2,1,0:T(4,128)} async-done(((f32[4096,3,128]{2,1,0:T(4,128)}), f32[4096,3,128]{2,1,0:T(4,128)}) %all-reduce.4.cloned.1.call-update) | async-done | bytes 6291472
  515.6 5.2 scatter_fusion.2
  520.8 2.7 scatter_fusion.3
  523.6 2.7 scatter_fusion.4
  528.6 3.4 fusion.54
  532.0 25.0 %scatter_fusion.5 = f32[1024,3,128]{2,1,0:T(4,128)} fusion(f32[1024,3,128]{2,1,0:T(4,128)} %fusion.54, s32[256]{0:T(256)S(1)} %bitcast.221, f32[256,3,128]{2,1,0:T(4,128)S(1)} %bitcast.207), kind=kCustom, calls=%fused_computation.15 | custom fusion | flops 98304 | bytes 1180672 | tf_op jit(solution)/shard_map/scatter-add | solution.py:86
  557.0 31.4 %scatter_fusion.6 = f32[1024,3,128]{2,1,0:T(4,128)} fusion(f32[1024,3,128]{2,1,0:T(4,128)} %scatter_fusion.5, s32[256]{0:T(256)S(1)} %reshape.560, f32[256,3,128]{2,1,0:T(4,128)S(1)} %bitcast.208), kind=kCustom, calls=%fused_computation.16 | custom fusion | flops 98304 | bytes 1180672 | tf_op jit(solution)/shard_map/scatter-add | solution.py:76
  588.4 16.5 %scatter_fusion.7 = f32[1024,3,128]{2,1,0:T(4,128)} fusion(f32[1024,3,128]{2,1,0:T(4,128)} %scatter_fusion.6, s32[128]{0:T(128)S(1)} %copy-done.17, f32[128,3,128]{2,1,0:T(4,128)S(1)} %bitcast.212), kind=kCustom, calls=%fused_computation.17 | custom fusion | flops 49152 | bytes 590336 | tf_op jit(solution)/shard_map/scatter-add | solution.py:76
  604.8 2.8 copy.50
  (591 shorter events, 359.5 us)
Async XLA Ops:
  6.5 10.7 %copy-start.2 = (f32[1024,128]{1,0:T(8,128)S(1)}, f32[1024,128]{1,0:T(8,128)}, u32[]{:S(2)}) copy-start(f32[1024,128]{1,0:T(8,128)} %param.15) | copy-start | bytes 1572868
  6.5 11.4 %copy-start.1 = (f32[1024,3,128]{2,0,1:T(8,128)S(1)}, f32[1024,3,128]{2,0,1:T(8,128)}, u32[]{:S(2)}) copy-start(f32[1024,3,128]{2,0,1:T(8,128)} %param.14) | copy-start | bytes 4718596
  6.5 10.7 %copy-start.18 = (s32[1,128]{1,0:T(1,128)S(1)}, s32[1,128]{1,0:T(1,128)}, u32[]{:S(2)}) copy-start(s32[1,128]{1,0:T(1,128)} %param.17) | copy-start | bytes 1540
  6.5 189.8 %all-gather.2.cloned.1.call-start = ((), (), s32[]{:S(2)}) async-start(), calls=%async_computation | async-start | bytes 8650752 | tf_op jit(solution)/shard_map/all_gather | solution.py:92
  11.1 8.4 %copy-start.15 = (s32[1,2,64]{2,1,0:T(2,128)S(1)}, s32[1,2,64]{2,1,0:T(2,128)}, u32[]{:S(2)}) copy-start(s32[1,2,64]{2,1,0:T(2,128)} %param.21) | copy-start | bytes 1540
  11.1 8.5 %copy-start.16 = (s32[1,2,64]{2,1,0:T(2,128)S(1)}, s32[1,2,64]{2,1,0:T(2,128)}, u32[]{:S(2)}) copy-start(s32[1,2,64]{2,1,0:T(2,128)} %param.20) | copy-start | bytes 1540
  11.2 9.1 %copy-start.8 = (s32[1,2,256]{2,1,0:T(2,128)S(1)}, s32[1,2,256]{2,1,0:T(2,128)}, u32[]{:S(2)}) copy-start(s32[1,2,256]{2,1,0:T(2,128)} %param.16) | copy-start | bytes 6148
  11.2 9.7 %copy-start.7 = (s32[1,32,8]{1,2,0:T(8,128)S(1)}, s32[1,32,8]{1,2,0:T(8,128)}, u32[]{:S(2)}) copy-start(s32[1,32,8]{1,2,0:T(8,128)} %param.19) | copy-start | bytes 3076
  11.9 183.5 %collective-permute-start = (f32[64,4,128]{2,0,1:T(8,128)}, f32[64,4,128]{2,0,1:T(8,128)S(1)}, u32[]{:S(2)}, u32[]{:S(2)}) collective-permute-start(f32[64,4,128]{2,0,1:T(8,128)} %get-tuple-element.247), channel_id=1, source_target_pairs={{0,32},{32,64},{64,96},{1,33},{33,65},{65,97},{2,34},{34,66},{66,9... | collective-permute-start | bytes 393224 | tf_op jit(solution)/shard_map/ppermute | solution.py:19
  15.9 179.5 %collective-permute-start.1 = (f32[64,4,128]{2,0,1:T(8,128)S(1)}, f32[64,4,128]{2,0,1:T(8,128)}, u32[]{:S(2)}, u32[]{:S(2)}) collective-permute-start(f32[64,4,128]{2,0,1:T(8,128)S(1)} %get-tuple-element.248), channel_id=1, source_target_pairs={{32,0},{64,32},{96,64},{33,1},{65,33},{97,65},{34,2},{66,34},{98,6... | collective-permute-start | bytes 393224 | tf_op jit(solution)/shard_map/ppermute | solution.py:21
  17.2 6.1 copy-start.13
  19.5 495.1 %all-reduce.4.cloned.1.call-start = ((), (), s32[]{:S(2)}) async-start(), calls=%async_computation.1 | async-start | bytes 16777216
  25.9 2.9 copy-start.9
  36.0 148.5 %copy-start.20 = (u32[128]{0:T(128)S(1)}, u32[128]{0:T(128)}, u32[]{:S(2)}) copy-start(u32[128]{0:T(128)} %constant.121) | copy-start | bytes 1540
  183.4 3.3 copy-start
  183.4 3.6 copy-start.10
  360.3 3.9 copy-start.4
  389.1 0.9 copy-start.5
  389.1 1.0 copy-start.19
  390.1 125.5 %copy-start.14 = (s32[128]{0:T(128)S(1)}, s32[128]{0:T(128)}, u32[]{:S(2)}) copy-start(s32[128]{0:T(128)} %copy-done.13) | copy-start | bytes 1540
  390.1 130.7 %copy-start.12 = (s32[64]{0:T(128)S(1)}, s32[64]{0:T(128)}, u32[]{:S(2)}) copy-start(s32[64]{0:T(128)} %get-tuple-element.252) | copy-start | bytes 772
  457.5 66.1 %copy-start.11 = (s32[64]{0:T(128)S(1)}, s32[64]{0:T(128)}, u32[]{:S(2)}) copy-start(s32[64]{0:T(128)} %get-tuple-element.251) | copy-start | bytes 772
  457.6 63.2 %collective-permute-start.2 = (f32[64,3,128]{2,1,0:T(4,128)S(1)}, f32[64,3,128]{2,1,0:T(4,128)S(1)}, u32[]{:S(2)}, u32[]{:S(2)}) collective-permute-start(f32[64,3,128]{2,1,0:T(4,128)S(1)} %bitcast.218), channel_id=1, source_target_pairs={{0,32},{32,64},{64,96},{1,33},{33,65},{65,97},{2,34},{34,66},{66,9... | collective-permute-start | bytes 294920 | tf_op jit(solution)/shard_map/ppermute | solution.py:19
  461.5 62.1 %collective-permute-start.3 = (f32[64,3,128]{2,1,0:T(4,128)S(1)}, f32[64,3,128]{2,1,0:T(4,128)S(1)}, u32[]{:S(2)}, u32[]{:S(2)}) collective-permute-start(f32[64,3,128]{2,1,0:T(4,128)S(1)} %bitcast.217), channel_id=1, source_target_pairs={{32,0},{64,32},{96,64},{33,1},{65,33},{97,65},{34,2},{66,34},{98,6... | collective-permute-start | bytes 294920 | tf_op jit(solution)/shard_map/ppermute | solution.py:21
  528.6 3.4 copy-start.3
  532.0 56.3 %copy-start.6 = (f32[8,16,3,128]{3,2,1,0:T(4,128)S(1)}, f32[8,16,3,128]{3,2,1,0:T(4,128)}, u32[]{:S(2)}) copy-start(f32[8,16,3,128]{3,2,1,0:T(4,128)} %get-tuple-element.129) | copy-start | bytes 589828
  532.0 56.3 %copy-start.17 = (s32[128]{0:T(128)S(1)}, s32[128]{0:T(128)}, u32[]{:S(2)}) copy-start(s32[128]{0:T(128)} %reshape.568) | copy-start | bytes 1540
Sparse Core Ops, SparseCore 0:
  19.6 57.6 all-gather.1
  389.3 125.2 all-reduce.3
where the time goes:
time: 620 us; the launch traced here: 615 us
  matrix products  230 us (37%)
  local copies, waits for them, and re-layouts  169 us (27%)
  other arithmetic  137 us (22%)
  waiting for transfers between devices  51.9 us (8%)
  between operations  14.5 us (2%)
  starting transfers between devices  10.5 us (2%)
    dot_general x40, matrix products, tile_forces(): jnp.einsum('pci,pcj->pij', own_points, far_centres, precision=highest)  96 us
    dot_general x40, matrix products, tile_forces(): jnp.einsum('pcj,pij->pci', far_centres, energy, precision=highest)  84.5 us
    gather x24, local copies, waits for them, and re-layouts, far_tiles(): return tile_forces(verts[target_idx], centroids(packed_rows[:, :3]), weight)  52.7 us
    unnamed x3, waiting for transfers between devices  51.9 us
    dot_general x40, matrix products, tile_forces(): jnp.einsum('pci,pij->pcj', own_points, energy, precision=highest)  49.1 us
    scatter-add x2, other arithmetic, remote(): return (pushed.at[clipped].add(push_far), react_far)  47.8 us
    gather x16, local copies, waits for them, and re-layouts, local_tiles(): centres[anchor_idx]  35.1 us
    scatter-add x1, other arithmetic, body(): pushed = jnp.zeros_like(verts).at[target_loc].add(push_loc)  25 us
  transfers between devices with their start and end apart: 6, of which 1 were waited for; matrix products, arithmetic and copies ran while one was open for 41% of the time, Pallas kernels for 0%

commit v1 on v0

v1 whole, which is shorter than its diff:
```python
import math

import jax
import jax.numpy as jnp
from jax import lax
from jax.experimental import pallas as pl
from jax.experimental.pallas import tpu as pltpu
from jax.sharding import PartitionSpec as P

f32 = jnp.float32
bf16 = jnp.bfloat16
i32 = jnp.int32
MESH = pl.DeviceIdType.MESH

NP = 1024
NV = 128
NB = 32
NS = 8
NF = 64
NR = NB * NS + 2 * NF
NL = 256
SQ = math.sqrt(math.log2(math.e))
FAR = 1.0e4
U = 4
DN = (((1,), (1,)), ((), ()))

vm = pl.BlockSpec(memory_space=pltpu.VMEM)
sm = pl.BlockSpec(memory_space=pltpu.SMEM)


def greet(me_t, me_b):
    sem = pltpu.get_barrier_semaphore()

    def one(o, c):
        pl.semaphore_signal(
            sem, inc=1, device_id=(me_t, lax.rem(me_b + o, NB)), device_id_type=MESH
        )
        return c

    lax.fori_loop(1, NB, one, 0)

    @pl.when(me_t > 0)
    def _():
        pl.semaphore_signal(sem, inc=1, device_id=(me_t - 1, me_b), device_id_type=MESH)

    @pl.when(me_t < 3)
    def _():
        pl.semaphore_signal(sem, inc=1, device_id=(me_t + 1, me_b), device_id_type=MESH)

    return sem


def greeted(sem, me_t):
    faces = (me_t > 0).astype(i32) + (me_t < 3).astype(i32)
    pl.semaphore_wait(sem, NB - 1 + faces)


def brick_copy(src, dst, s_sem, r_sem, me_t, me_b, o):
    peer = lax.rem(me_b + o, NB)
    return pltpu.make_async_remote_copy(
        src_ref=src.at[peer],
        dst_ref=dst.at[me_b],
        send_sem=s_sem.at[peer],
        recv_sem=r_sem.at[me_b],
        device_id=(me_t, peer),
        device_id_type=MESH,
    )


def brick_arrival(src, dst, s_sem, r_sem, me_t, me_b, o):
    peer = lax.rem(me_b + o, NB)
    return pltpu.make_async_remote_copy(
        src_ref=src.at[peer],
        dst_ref=dst.at[peer],
        send_sem=s_sem.at[peer],
        recv_sem=r_sem.at[peer],
        device_id=(me_t, peer),
        device_id_type=MESH,
    )


def face_copy(src, dst, s_sem, r_sem, me_t, me_b, side):
    step = -1 if side == 0 else 1
    return pltpu.make_async_remote_copy(
        src_ref=src.at[side],
        dst_ref=dst.at[1 - side],
        send_sem=s_sem.at[side],
        recv_sem=r_sem.at[1 - side],
        device_id=(me_t + step, me_b),
        device_id_type=MESH,
    )


def face_arrival(src, dst, s_sem, r_sem, me_t, me_b, side):
    step = -1 if side == 0 else 1
    return pltpu.make_async_remote_copy(
        src_ref=src.at[side],
        dst_ref=dst.at[side],
        send_sem=s_sem.at[side],
        recv_sem=r_sem.at[side],
        device_id=(me_t + step, me_b),
        device_id_type=MESH,
    )


def finish(src_b, dst_b, src_f, dst_f, sb, rb, sf, rf, me_t, me_b):
    def one(o, c):
        brick_arrival(src_b, dst_b, sb, rb, me_t, me_b, o).wait_recv()
        brick_copy(src_b, dst_b, sb, rb, me_t, me_b, o).wait_send()
        return c

    lax.fori_loop(1, NB, one, 0)
    for side in range(2):

        @pl.when((me_t > 0) if side == 0 else (me_t < 3))
        def _(side=side):
            face_arrival(src_f, dst_f, sf, rf, me_t, me_b, side).wait_recv()
            face_copy(src_f, dst_f, sf, rf, me_t, me_b, side).wait_send()


def ask_kernel(rp, rs, fp, verts, got_b, got_f, out_b, out_f, sb, rb, sf, rf):
    me_t = lax.axis_index("slab")
    me_b = lax.axis_index("brick")
    sem = greet(me_t, me_b)

    def row(idx):
        return jnp.where(idx >= 0, verts[jnp.maximum(idx, 0)], FAR)

    def fill_face(k, c):
        for side in range(2):
            idx = fp[side, k]
            out_f[side, k, 0:3] = row(idx)
            out_f[side, k, 3:4] = jnp.full((1, NV), jnp.minimum(idx, 0).astype(f32))
        return c

    lax.fori_loop(0, NF, fill_face, 0)
    none = jnp.full((NS, 1, NV), -1.0, f32)
    got_b[me_b, :, 0:3, :] = jnp.full((NS, 3, NV), FAR, f32)
    got_b[me_b, :, 3:4, :] = none

    @pl.when(me_t == 0)
    def _():
        got_f[0] = jnp.full((NF, 4, NV), -1.0, f32)

    @pl.when(me_t == 3)
    def _():
        got_f[1] = jnp.full((NF, 4, NV), -1.0, f32)

    greeted(sem, me_t)
    for side in range(2):

        @pl.when((me_t > 0) if side == 0 else (me_t < 3))
        def _(side=side):
            face_copy(out_f, got_f, sf, rf, me_t, me_b, side).start()

    def send(o, c):
        s = lax.rem(me_b + o, NB)
        for k in range(NS):
            idx = rp[s, k]
            out_b[s, k, 0:3] = row(idx)
            src = jnp.where(idx >= 0, rs[s, k], -1)
            out_b[s, k, 3:4] = jnp.full((1, NV), src.astype(f32))
        brick_copy(out_b, got_b, sb, rb, me_t, me_b, o).start()
        return c

    lax.fori_loop(1, NB, send, 0)
    finish(out_b, got_b, out_f, got_f, sb, rb, sf, rf, me_t, me_b)


def ask(rp, rs, fp, verts):
    return pl.pallas_call(
        ask_kernel,
        name="ask",
        out_shape=(
            jax.ShapeDtypeStruct((NB, NS, 4, NV), f32),
            jax.ShapeDtypeStruct((2, NF, 4, NV), f32),
        ),
        in_specs=[sm, sm, sm, vm],
        out_specs=(vm, vm),
        scratch_shapes=[
            pltpu.VMEM((NB, NS, 4, NV), f32),
            pltpu.VMEM((2, NF, 4, NV), f32),
            pltpu.SemaphoreType.DMA((NB,)),
            pltpu.SemaphoreType.DMA((NB,)),
            pltpu.SemaphoreType.DMA((2,)),
            pltpu.SemaphoreType.DMA((2,)),
        ],
        compiler_params=pltpu.CompilerParams(collective_id=0, has_side_effects=True),
    )(rp, rs, fp, verts)


def give_kernel(out_b, out_f, got_b, got_f, sb, rb, sf, rf):
    me_t = lax.axis_index("slab")
    me_b = lax.axis_index("brick")
    sem = greet(me_t, me_b)
    got_b[me_b] = jnp.zeros((NS, 3, NV), f32)

    @pl.when(me_t == 0)
    def _():
        got_f[0] = jnp.zeros((NF, 3, NV), f32)

    @pl.when(me_t == 3)
    def _():
        got_f[1] = jnp.zeros((NF, 3, NV), f32)

    greeted(sem, me_t)
    for side in range(2):

        @pl.when((me_t > 0) if side == 0 else (me_t < 3))
        def _(side=side):
            face_copy(out_f, got_f, sf, rf, me_t, me_b, side).start()

    def send(o, c):
        brick_copy(out_b, got_b, sb, rb, me_t, me_b, o).start()
        return c

    lax.fori_loop(1, NB, send, 0)
    finish(out_b, got_b, out_f, got_f, sb, rb, sf, rf, me_t, me_b)


def give(out_b, out_f):
    return pl.pallas_call(
        give_kernel,
        name="give",
        out_shape=(
            jax.ShapeDtypeStruct((NB, NS, 3, NV), f32),
            jax.ShapeDtypeStruct((2, NF, 3, NV), f32),
        ),
        in_specs=[vm, vm],
        out_specs=(vm, vm),
        scratch_shapes=[
            pltpu.SemaphoreType.DMA((NB,)),
            pltpu.SemaphoreType.DMA((NB,)),
            pltpu.SemaphoreType.DMA((2,)),
            pltpu.SemaphoreType.DMA((2,)),
        ],
        compiler_params=pltpu.CompilerParams(collective_id=1, has_side_effects=True),
    )(out_b, out_f)


def split(x):
    high = x.astype(bf16).astype(f32)
    return high, x - high


def ahead(v, k):
    return pltpu.roll(v, NV - k, 1)


def energies(xs, vs, stiff, e_ij, e_ji):
    one = jnp.ones((8, NV), f32)
    zero = jnp.zeros((8, NV), f32)
    cs = [(v + ahead(v, 1) + ahead(v, 2)) * (1.0 / 3.0) for v in vs]
    xp = [x * SQ for x in xs]
    cp = [c * SQ for c in cs]
    x1, x2 = zip(*[split(x) for x in xp])
    c1, c2 = zip(*[split(c) for c in cp])
    n = -0.5 * (xp[0] * xp[0] + xp[1] * xp[1] + xp[2] * xp[2])
    m = -0.5 * (cp[0] * cp[0] + cp[1] * cp[1] + cp[2] * cp[2]) + jnp.log2(stiff) - 7.0
    n1, r = split(n)
    n2, n3 = split(r)
    m1, r = split(m)
    m2, m3 = split(r)
    a = jnp.concatenate([*x1, *x1, *x2, n1, n2, n3, one, one, one, zero], 0).astype(bf16)
    b = jnp.concatenate([*c1, *c2, *c1, one, one, one, m1, m2, m3, zero], 0).astype(bf16)
    at = a.T
    lx = jnp.concatenate([*x1, *x2, one, zero], 0).astype(bf16)
    lc = jnp.concatenate([*c1, *c2, one, zero], 0).astype(bf16)
    sub = lax.broadcasted_iota(i32, (NV, NV), 0) % 8
    for q in range(0, 8, 2):
        bq = jnp.concatenate([jnp.where(sub == q + k, b, jnp.zeros_like(b)) for k in range(2)], 1)
        e = jnp.exp2(jnp.dot(at, bq, preferred_element_type=f32))
        eh = e.astype(bf16)
        el = (e - eh.astype(f32)).astype(bf16)
        e_ij[0:NV, q * NV : (q + 2) * NV] = eh
        e_ij[NV : 2 * NV, q * NV : (q + 2) * NV] = el
        for k in range(2):
            o = (q + k) * NV
            e_ji[o : o + NV, 0:NV] = eh[:, k * NV : (k + 1) * NV]
            e_ji[o : o + NV, NV : 2 * NV] = el[:, k * NV : (k + 1) * NV]
    return xs, cs, lx, lc


def diagonal(r):
    sub = lax.broadcasted_iota(i32, (8, NV), 0)
    out = []
    for k in range(7):
        o = r[8 * k : 8 * k + 8, 0:NV]
        for q in range(1, 8):
            o = jnp.where(sub == q, r[8 * k : 8 * k + 8, q * NV : (q + 1) * NV], o)
        out.append(o)
    return out


def forces(xs, cs, lx, lc, e_ij, e_ji):
    rx = diagonal(jnp.dot(jnp.concatenate([lx, lx], 1), e_ij[...], preferred_element_type=f32))
    rc = diagonal(
        lax.dot_general(
            jnp.concatenate([lc, lc], 1), e_ji[...], DN, preferred_element_type=f32
        )
    )
    inv = 1.0 / SQ
    react = [cs[k] * rx[6] - (rx[k] + rx[3 + k]) * inv for k in range(3)]
    push = [xs[k] * rc[6] - (rc[k] + rc[3 + k]) * inv for k in range(3)]
    return push, react


def pair_kernel(
    loc, pick, fpick, src, verts, stiff, got_b, got_f,
    acc_p, acc_r, back_b, back_f,
    order, xg, vg, sg, pg, rg, e_ij, e_ji, far, back,
):
    def clear(i, c):
        acc_p[pl.ds(i * 16, 16)] = jnp.zeros((16, 3, NV), f32)
        acc_r[pl.ds(i * 16, 16)] = jnp.zeros((16, 3, NV), f32)
        return c

    lax.fori_loop(0, NP // 16, clear, 0)

    def load(i, c):
        far[pl.ds(i * NS, NS)] = got_b[i]
        return c

    lax.fori_loop(0, NB, load, 0)
    for side in range(2):
        far[pl.ds(NB * NS + side * NF, NF)] = got_f[side]
    far[NR] = jnp.full((4, NV), FAR, f32)

    def count(i, n):
        order[n] = i
        return n + (src[i] >= 0).astype(i32)

    n = lax.fori_loop(0, NR, count, jnp.int32(0))

    def pad(i, c):
        order[n + i] = NR
        return c

    lax.fori_loop(0, 8 * U, pad, 0)

    def block(get_x, get_b, put):
        kept = []

        def last(u):
            push, react = forces(*kept[u], e_ij.at[u], e_ji.at[u])
            for c in range(3):
                pg[u, :, c, :] = push[c]
                rg[u, :, c, :] = react[c]

        where = []
        for u in range(U):
            for p in range(8):
                x = get_x(u * 8 + p)
                b = get_b(u * 8 + p)
                where.append(b)
                xg[u, p] = x
                vg[u, p] = verts[b]
                sg[u, pl.ds(p, 1), :] = stiff[pl.ds(b, 1), :]
        for u in range(U):
            xs = [xg[u, :, c, :] for c in range(3)]
            vs = [vg[u, :, c, :] for c in range(3)]
            kept.append(energies(xs, vs, sg[u], e_ij.at[u], e_ji.at[u]))
            if u > 0:
                last(u - 1)
        last(U - 1)
        for u in range(U):
            for p in range(8):
                put(u * 8 + p, pg[u, p])
                acc_r[where[u * 8 + p]] += rg[u, p]

    def local_step(g, c):
        base = g * 8 * U

        def put(i, v):
            acc_p[loc[0, base + i]] += v

        block(lambda i: verts[loc[0, base + i]], lambda i: loc[1, base + i], put)
        return c

    lax.fori_loop(0, NL // (8 * U), local_step, 0)

    def far_step(g, c):
        base = g * 8 * U

        def get_b(i):
            o = order[base + i]
            s = jnp.maximum(src[o], 0)
            brick = pick[jnp.minimum(s, NV - 1)]
            j = jnp.clip(o - NB * NS, 0, 2 * NF - 1)
            face = fpick[j]
            return jnp.where(o < NB * NS, brick, face)

        def put(i, v):
            back[order[base + i]] = v

        block(lambda i: far[order[base + i], 0:3], get_b, put)
        return c

    lax.fori_loop(0, (n + 8 * U - 1) // (8 * U), far_step, 0)

    def store(i, c):
        back_b[i] = back[pl.ds(i * NS, NS)]
        return c

    lax.fori_loop(0, NB, store, 0)
    for side in range(2):
        back_f[side] = back[pl.ds(NB * NS + side * NF, NF)]


def pairs(loc, pick, fpick, src, verts, stiff, got_b, got_f):
    acc = jax.ShapeDtypeStruct((NP, 3, NV), f32)
    return pl.pallas_call(
        pair_kernel,
        name="pairs",
        out_shape=(
            acc,
            acc,
            jax.ShapeDtypeStruct((NB, NS, 3, NV), f32),
            jax.ShapeDtypeStruct((2, NF, 3, NV), f32),
        ),
        in_specs=[sm] * 4 + [vm] * 4,
        out_specs=(vm,) * 4,
        scratch_shapes=[
            pltpu.SMEM((NR + 8 * U,), i32),
            pltpu.VMEM((U, 8, 3, NV), f32),
            pltpu.VMEM((U, 8, 3, NV), f32),
            pltpu.VMEM((U, 8, NV), f32),
            pltpu.VMEM((U, 8, 3, NV), f32),
            pltpu.VMEM((U, 8, 3, NV), f32),
            pltpu.VMEM((U, 2 * NV, 8 * NV), bf16),
            pltpu.VMEM((U, 8 * NV, 2 * NV), bf16),
            pltpu.VMEM((NR + 1, 4, NV), f32),
            pltpu.VMEM((NR + 1, 3, NV), f32),
        ],
        compiler_params=pltpu.CompilerParams(vmem_limit_bytes=48 << 20),
    )(loc, pick, fpick, src, verts, stiff, got_b, got_f)


def merge_kernel(rp, fp, acc_p, acc_r, got_b, got_f, out):
    def spread(i, c):
        for h in range(2):
            at = pl.ds(i * 16 + h * 8, 8)
            r = acc_r[at]
            s = r + pltpu.roll(r, 1, 2) + pltpu.roll(r, 2, 2)
            out[at] = acc_p[at] + s * (1.0 / 3.0)
        return c

    lax.fori_loop(0, NP // 16, spread, 0)

    def brick(s, c):
        for k in range(NS):
            idx = rp[s, k]

            @pl.when(idx >= 0)
            def _(k=k, idx=idx):
                out[idx] += got_b[s, k]

        return c

    lax.fori_loop(0, NB, brick, 0)
    me_t = lax.axis_index("slab")

    def face(k, c):
        for side in range(2):
            idx = fp[side, k]
            there = (me_t > 0) if side == 0 else (me_t < 3)

            @pl.when((idx >= 0) & there)
            def _(side=side, idx=idx):
                out[idx] += got_f[side, k]

        return c

    lax.fori_loop(0, NF, face, 0)


def merge(rp, fp, acc_p, acc_r, got_b, got_f):
    return pl.pallas_call(
        merge_kernel,
        name="merge",
        out_shape=jax.ShapeDtypeStruct((NP, 3, NV), f32),
        in_specs=[sm] * 2 + [vm] * 4,
        out_specs=vm,
        compiler_params=pltpu.CompilerParams(vmem_limit_bytes=48 << 20),
    )(rp, fp, acc_p, acc_r, got_b, got_f)


def body(verts, stiffness, local_pairs, border_pick, recv_src, recv_pair, face_pick, face_pair):
    rp = recv_pair[0]
    fp = face_pair[0]
    got_b, got_f = ask(rp, recv_src[0], fp, verts)
    src = jnp.concatenate([got_b[:, :, 3, 0].reshape(-1), got_f[:, :, 3, 0].reshape(-1)])
    acc_p, acc_r, back_b, back_f = pairs(
        local_pairs[0],
        border_pick[0],
        face_pick[0].reshape(-1),
        src.astype(i32),
        verts,
        stiffness,
        got_b,
        got_f,
    )
    ret_b, ret_f = give(back_b, back_f)
    return merge(rp, fp, acc_p, acc_r, ret_b, ret_f)


def solution(mesh):
    both = ("slab", "brick")
    placed = (
        P(both, None, None),
        P(both, None),
        P(both, None, None),
        P(both, None),
        P(both, None, None),
        P(both, None, None),
        P(both, None, None),
        P(both, None, None),
    )
    return jax.shard_map(
        body, mesh=mesh, in_specs=placed, out_specs=P(both, None, None), check_vma=False
    )
```

time: 620 us -> 98.5 us (0.16)
  the two profiles are of different devices: /device:TPU:1 before, /device:TPU:17 now
where the time goes in v1:
time: 98.5 us; the launch traced here: 97.9 us
  Pallas kernels  80.5 us (82%)
  local copies, waits for them, and re-layouts  17.3 us (18%)
    pallas_call x1, Pallas kernels, pairs(): pl.pallas_call(pair_kernel, name='pairs', out_shape=(acc, acc, jax.ShapeD...  29.1 us
    pallas_call x1, Pallas kernels, give(): pl.pallas_call(give_kernel, name='give', out_shape=(jax.ShapeDtypeStruct(...  20.5 us
    pallas_call x1, Pallas kernels, ask(): pl.pallas_call(ask_kernel, name='ask', out_shape=(jax.ShapeDtypeStruct((N...  18.6 us
    pallas_call x1, Pallas kernels, merge(): pl.pallas_call(merge_kernel, name='merge', out_shape=jax.ShapeDtypeStruct...  12.3 us
    unnamed x25, local copies, waits for them, and re-layouts  12 us

profile of v1, /device:TPU:17, one launch (start us, length us, event | category | flops | bytes accessed | tf_op | source)
XLA Modules:
  0.0 97.9 jit_solution(15033736408692543207)
XLA Ops:
  0.0 0.8 reshape_squeeze.9.fpick
  0.8 1.4 %copy.15 = s32[1,32,8]{2,1,0:T(8,128)} copy(s32[1,32,8]{1,2,0:T(8,128)} %param.12) | data formatting | bytes 2048 | tf_op args[4]
  2.1 1.4 %copy.14 = s32[1,32,8]{2,1,0:T(8,128)} copy(s32[1,32,8]{1,2,0:T(8,128)} %param.13) | data formatting | bytes 2048 | tf_op args[5]
  3.5 3.8 %copy.16.verts = f32[1024,3,128]{2,1,0:T(4,128)} copy(f32[1024,3,128]{2,0,1:T(8,128)} %param.8) | data formatting | bytes 3145728 | tf_op args[0]
  7.3 0.0 copy-start.1
  7.3 0.0 copy-start.9
  7.3 0.0 copy-start.10
  7.3 18.6 %ask.1 = (f32[32,8,4,128]{3,2,1,0:T(4,128)}, f32[2,64,4,128]{3,2,1,0:T(4,128)}) custom-call(s32[32,8]{1,0:T(8,128)} %bitcast.5, s32[32,8]{1,0:T(8,128)} %bitcast.11, s32[2,64]{1,0:T(2,128)} %bitcast.7, f32[1024,3,128]{2,1,0:T(4,128)} %copy.16.verts), custom_call_target="tpu_custom_call" | custom-call | tf_op jit(solution)/shard_map/ask/pallas_call | solution.py:171
  25.8 1.5 %slice_reduce_fusion.1 = f32[2,64]{1,0:T(2,128)S(1)} fusion(f32[2,64,4,128]{3,2,1,0:T(4,128)} %get-tuple-element.14.got_f), kind=kLoop, calls=%fused_computation.1 | loop fusion | bytes 1024 | tf_op jit(solution)/shard_map/slice | solution.py:492
  27.4 0.1 reshape_squeeze.11
  27.4 1.6 %slice_reduce_fusion = f32[32,8]{1,0:T(8,128)S(1)} fusion(f32[32,8,4,128]{3,2,1,0:T(4,128)} %get-tuple-element.13.got_b), kind=kLoop, calls=%fused_computation | loop fusion | bytes 2048 | tf_op jit(solution)/shard_map/slice | solution.py:492
  29.1 0.1 reshape_squeeze.10
  29.2 0.0 copy-done.1
  29.2 0.0 copy-done.9
  29.2 0.0 copy-done.10
  29.2 0.0 copy-start
  29.2 1.0 %copy-done = f32[32,8,4,128]{3,2,1,0:T(4,128)S(1)} copy-done((f32[32,8,4,128]{3,2,1,0:T(4,128)S(1)}, f32[32,8,4,128]{3,2,1,0:T(4,128)}, u32[]{:S(2)}) %copy-start) | copy-done | bytes 524312
  30.2 0.0 copy-start.4
  30.2 0.9 copy-done.4
  31.2 0.0 copy-start.7
  31.2 0.0 copy-start.8
  31.2 29.1 %pairs.1 = (f32[1024,3,128]{2,1,0:T(4,128)S(1)}, f32[1024,3,128]{2,1,0:T(4,128)}, f32[32,8,3,128]{3,2,1,0:T(4,128)S(1)}, f32[2,64,3,128]{3,2,1,0:T(4,128)S(1)}) custom-call(s32[2,256]{1,0:T(2,128)S(1)} %bitcast.9, s32[128]{0:T(128)S(1)} %bitcast.10, s32[128]{0:T(128)S(1)} %reshape_squeeze.9.fpick, s32[384]{0:T(512)S(1)} %maximum_convert_fusion.src, ...), custom_call_target="tpu_custom_call" | custom-call | tf_op jit(solution)/shard_map/pairs/pallas_call | solution.py:412
  60.3 0.8 copy-done.2
  61.1 0.7 copy-done.5
  61.8 20.5 %give.1 = (f32[32,8,3,128]{3,2,1,0:T(4,128)}, f32[2,64,3,128]{3,2,1,0:T(4,128)}) custom-call(f32[32,8,3,128]{3,2,1,0:T(4,128)} %copy-done.2, f32[2,64,3,128]{3,2,1,0:T(4,128)} %copy-done.5), custom_call_target="tpu_custom_call" | custom-call | tf_op jit(solution)/shard_map/give/pallas_call | solution.py:222
  82.4 0.0 copy-done.7
  82.4 0.0 copy-done.8
  82.4 0.0 copy-start.3
  82.4 1.0 %copy-done.3 = f32[32,8,3,128]{3,2,1,0:T(4,128)S(1)} copy-done((f32[32,8,3,128]{3,2,1,0:T(4,128)S(1)}, f32[32,8,3,128]{3,2,1,0:T(4,128)}, u32[]{:S(2)}) %copy-start.3) | copy-done | bytes 393240
  83.4 0.9 copy-done.6
  84.4 12.3 %merge.1 = f32[1024,3,128]{2,1,0:T(4,128)S(1)} custom-call(s32[32,8]{1,0:T(8,128)S(1)} %bitcast.6, s32[2,64]{1,0:T(2,128)S(1)} %bitcast.8, f32[1024,3,128]{2,1,0:T(4,128)S(1)} %get-tuple-element.15.acc_p, f32[1024,3,128]{2,1,0:T(4,128)} %get-tuple-element.16.acc_r, f32[32,8,3,128]{3,2,1,0:T(4,128)S(1)} %copy-done.3, f32[2,64,3,128]{3,2,1,0:T(4,128)S(1)} %copy-done.6), custom_call_target="tpu_custom_call" | custom-call | tf_op jit(solution)/shard_map/merge/pallas_call | solution.py:478
  96.7 1.2 %copy.18 = f32[1024,3,128]{2,0,1:T(8,128)} copy(f32[1024,3,128]{2,1,0:T(4,128)S(1)} %merge.1) | data formatting | bytes 3145728 | tf_op jit(solution)/shard_map/merge/pallas_call | solution.py:478
  (4 shorter events, 0.0 us)
Async XLA Ops:
  7.3 21.9 %copy-start.1 = (f32[1024,128]{1,0:T(8,128)S(1)}, f32[1024,128]{1,0:T(8,128)}, u32[]{:S(2)}) copy-start(f32[1024,128]{1,0:T(8,128)} %stiff.1) | copy-start | bytes 1572868
  7.3 21.9 %copy-start.9 = (s32[1,2,256]{2,1,0:T(2,128)S(1)}, s32[1,2,256]{2,1,0:T(2,128)}, u32[]{:S(2)}) copy-start(s32[1,2,256]{2,1,0:T(2,128)} %param.10) | copy-start | bytes 6148
  7.3 21.9 %copy-start.10 = (s32[1,128]{1,0:T(1,128)S(1)}, s32[1,128]{1,0:T(1,128)}, u32[]{:S(2)}) copy-start(s32[1,128]{1,0:T(1,128)} %param.11) | copy-start | bytes 1540
  29.2 1.0 %copy-start = (f32[32,8,4,128]{3,2,1,0:T(4,128)S(1)}, f32[32,8,4,128]{3,2,1,0:T(4,128)}, u32[]{:S(2)}) copy-start(f32[32,8,4,128]{3,2,1,0:T(4,128)} %get-tuple-element.13.got_b) | copy-start | bytes 1572868
  30.2 0.9 copy-start.4
  31.2 51.2 %copy-start.7 = (s32[1,32,8]{2,1,0:T(8,128)S(1)}, s32[1,32,8]{2,1,0:T(8,128)}, u32[]{:S(2)}) copy-start(s32[1,32,8]{2,1,0:T(8,128)} %copy.14) | copy-start | bytes 3076
  31.2 51.2 %copy-start.8 = (s32[1,2,64]{2,1,0:T(2,128)S(1)}, s32[1,2,64]{2,1,0:T(2,128)}, u32[]{:S(2)}) copy-start(s32[1,2,64]{2,1,0:T(2,128)} %param.15) | copy-start | bytes 1540
  60.3 0.8 copy-start.2
  61.1 0.7 copy-start.5
  82.4 1.0 %copy-start.3 = (f32[32,8,3,128]{3,2,1,0:T(4,128)S(1)}, f32[32,8,3,128]{3,2,1,0:T(4,128)}, u32[]{:S(2)}) copy-start(f32[32,8,3,128]{3,2,1,0:T(4,128)} %get-tuple-element.19.got_b) | copy-start | bytes 1179652
  83.4 0.9 copy-start.6

commit v2 on v0

v2 whole, which is shorter than its diff:
```python
import math

import jax
import jax.numpy as jnp
from jax import lax
from jax.experimental import pallas as pl
from jax.experimental.pallas import tpu as pltpu
from jax.sharding import PartitionSpec as P

f32 = jnp.float32
bf16 = jnp.bfloat16
i32 = jnp.int32
MESH = pl.DeviceIdType.MESH

NP = 1024
NV = 128
NB = 32
NS = 8
NF = 64
NBS = NB * NS
NL = 256
FIRST = 20
SQ = math.sqrt(math.log2(math.e))
FAR = 1.0e4
U = 4
LAG = 4
DN = (((1,), (1,)), ((), ()))
D0 = (((0,), (0,)), ((), ()))

vm = pl.BlockSpec(memory_space=pltpu.VMEM)
sm = pl.BlockSpec(memory_space=pltpu.SMEM)


def greet(me_t, me_b):
    sem = pltpu.get_barrier_semaphore()

    def one(o, c):
        pl.semaphore_signal(
            sem, inc=1, device_id=(me_t, lax.rem(me_b + o, NB)), device_id_type=MESH
        )
        return c

    lax.fori_loop(1, NB, one, 0)

    @pl.when(me_t > 0)
    def _():
        pl.semaphore_signal(sem, inc=1, device_id=(me_t - 1, me_b), device_id_type=MESH)

    @pl.when(me_t < 3)
    def _():
        pl.semaphore_signal(sem, inc=1, device_id=(me_t + 1, me_b), device_id_type=MESH)

    return sem


def greeted(sem, me_t):
    faces = (me_t > 0).astype(i32) + (me_t < 3).astype(i32)
    pl.semaphore_wait(sem, NB - 1 + faces)


class Brick:
    def __init__(self, src, dst, s_sem, r_sem, me_t, me_b):
        self.a = (src, dst, s_sem, r_sem, me_t, me_b)

    def copy(self, o, arrival=False):
        src, dst, s_sem, r_sem, me_t, me_b = self.a
        peer = lax.rem(me_b + o, NB)
        at = peer if arrival else me_b
        return pltpu.make_async_remote_copy(
            src_ref=src.at[peer],
            dst_ref=dst.at[at],
            send_sem=s_sem.at[peer],
            recv_sem=r_sem.at[at],
            device_id=(me_t, peer),
            device_id_type=MESH,
        )

    def start(self):
        def one(o, c):
            self.copy(o).start()
            return c

        lax.fori_loop(1, NB, one, 0)

    def wait(self):
        def one(o, c):
            self.copy(o, True).wait_recv()
            self.copy(o).wait_send()
            return c

        lax.fori_loop(1, NB, one, 0)


class Face:
    def __init__(self, src, dst, s_sem, r_sem, me_t, me_b):
        self.a = (src, dst, s_sem, r_sem, me_t, me_b)

    def copy(self, side, arrival=False):
        src, dst, s_sem, r_sem, me_t, me_b = self.a
        at = side if arrival else 1 - side
        return pltpu.make_async_remote_copy(
            src_ref=src.at[side],
            dst_ref=dst.at[at],
            send_sem=s_sem.at[side],
            recv_sem=r_sem.at[at],
            device_id=(me_t + (1 if side else -1), me_b),
            device_id_type=MESH,
        )

    def there(self, side):
        return (self.a[4] < 3) if side else (self.a[4] > 0)

    def start(self):
        for side in range(2):

            @pl.when(self.there(side))
            def _(side=side):
                self.copy(side).start()

    def wait(self):
        for side in range(2):

            @pl.when(self.there(side))
            def _(side=side):
                self.copy(side, True).wait_recv()
                self.copy(side).wait_send()


def split(x):
    high = x.astype(bf16).astype(f32)
    return high, x - high


def ahead(v, k):
    return pltpu.roll(v, NV - k, 1)


def prepare(xs, vs, stiff, lx, lc):
    one = jnp.ones((8, NV), f32)
    zero = jnp.zeros((8, NV), f32)
    cs = [(v + ahead(v, 1) + ahead(v, 2)) * (1.0 / 3.0) for v in vs]
    xp = [x * SQ for x in xs]
    cp = [c * SQ for c in cs]
    x1, x2 = zip(*[split(x) for x in xp])
    c1, c2 = zip(*[split(c) for c in cp])
    n = -0.5 * (xp[0] * xp[0] + xp[1] * xp[1] + xp[2] * xp[2])
    m = -0.5 * (cp[0] * cp[0] + cp[1] * cp[1] + cp[2] * cp[2]) + jnp.log2(stiff) - 7.0
    n1, r = split(n)
    n2, n3 = split(r)
    m1, r = split(m)
    m2, m3 = split(r)
    a = jnp.concatenate([*x1, *x1, *x2, n1, n2, n3, one, one, one, zero], 0).astype(bf16)
    b = jnp.concatenate([*c1, *c2, *c1, one, one, one, m1, m2, m3, zero], 0).astype(bf16)
    for ref, rows in ((lx, [*x1, *x2, one, zero]), (lc, [*c1, *c2, one, zero])):
        for k, r in enumerate(rows):
            ref[pl.ds(k, 8, stride=8), :] = r
    return cs, a.T, b


def energies(at, b, t):
    sub = lax.broadcasted_iota(i32, (NV, NV), 0) % 8
    zero = jnp.zeros_like(b)
    two = jnp.concatenate([jnp.where(sub == 2 * t + k, b, zero) for k in range(2)], 1)
    e = jnp.exp2(jnp.dot(at, two, preferred_element_type=f32))
    high = e.astype(bf16)
    return high, (e - high.astype(f32)).astype(bf16)


def sums(t, e, lx, lc, rx, rc):
    h0, l0, h1, l1 = e
    rows = slice(16 * t, 16 * t + 16)
    x = lx[rows, :].astype(bf16)
    c = lc[rows, :].astype(bf16)
    cat = jnp.concatenate
    e_ij = cat([cat([h0, h1], 1), cat([l0, l1], 1)], 0)
    e_ji = cat([cat([h0, l0], 1), cat([h1, l1], 1)], 0)
    r = jnp.dot(cat([x, x], 1), e_ij, preferred_element_type=f32)
    s = lax.dot_general(cat([c, c], 1), e_ji, DN, preferred_element_type=f32)
    for ref, v in ((rx, r), (rc, s)):
        ref[16 * t : 16 * t + 8, :] = v[0:8, 0:NV]
        ref[16 * t + 8 : 16 * t + 16, :] = v[8:16, NV : 2 * NV]


def forces(xs, cs, rx, rc):
    def get(ref, k):
        return ref[pl.ds(k, 8, stride=8), :]

    inv = 1.0 / SQ
    q = get(rx, 6)
    r = get(rc, 6)
    react = [cs[k] * q - (get(rx, k) + get(rx, 3 + k)) * inv for k in range(3)]
    push = [xs[k] * r - (get(rc, k) + get(rc, 3 + k)) * inv for k in range(3)]
    return push, react


class Groups:
    def __init__(self, xg, vg, sg, lx, lc, rx, rc, eb):
        self.r = (xg, vg, sg, lx, lc, rx, rc, eb)

    def run(self, first, count, load, put):
        xg, vg, sg, lx, lc, rx, rc, eb = self.r
        n = U * 4

        def second(i, g):
            u, t = divmod(i, 4)
            e = [eb[u, t, k] for k in range(4)]
            sums(t, e, lx.at[u], lc.at[u], rx.at[u], rc.at[u])
            if t == 3:
                xs = [xg[u, c] for c in range(3)]
                cs = [vg[u, c] for c in range(3)]
                put(g, *forces(xs, cs, rx.at[u], rc.at[u]))

        def step(s, carry):
            base = first + s * U
            for i in range(n):
                u, t = divmod(i, 4)
                if t == 0:
                    load(u, base + u)
                    xs = [xg[u, c] for c in range(3)]
                    cs, at, b = prepare(xs, [vg[u, c] for c in range(3)], sg[u], lx.at[u], lc.at[u])
                    for c in range(3):
                        vg[u, c] = cs[c]
                j = i - LAG
                ju = (j % n) // 4
                second(j % n, base + ju if j >= 0 else jnp.maximum(base + ju - U, first))
                high, low = energies(at, b, t)
                eb[u, t, 0] = high[:, :NV]
                eb[u, t, 1] = low[:, :NV]
                eb[u, t, 2] = high[:, NV:]
                eb[u, t, 3] = low[:, NV:]
            return carry

        lax.fori_loop(0, count // U, step, 0)
        for j in range(n - LAG, n):
            second(j, first + count - U + j // 4)


def rows8(g, base=0):
    return pl.ds(pl.multiple_of(base + g * 8, 8), 8)


def pair_kernel(
    rp, fp, loc, pick, fpick, rs, verts, stiff,
    push_l, react, ret_b, ret_f, meta,
    got_b, got_f, out_b, out_f, back_b, back_f, brd, gv,
    xg, vg, sg, lx, lc, rx, rc, eb, sems, fsems,
):
    me_t = lax.axis_index("slab")
    me_b = lax.axis_index("brick")
    barrier = greet(me_t, me_b)
    ask_b = Brick(out_b, got_b, sems.at[0], sems.at[1], me_t, me_b)
    ask_f = Face(out_f, got_f, fsems.at[0], fsems.at[1], me_t, me_b)
    give_b = Brick(back_b, ret_b, sems.at[2], sems.at[3], me_t, me_b)
    give_f = Face(back_f, ret_f, fsems.at[2], fsems.at[3], me_t, me_b)

    def row(c, idx):
        return jnp.where(idx >= 0, verts[c, pl.ds(jnp.maximum(idx, 0), 1), :], FAR)

    def fill_brick(s, carry):
        for k in range(NS):
            idx = rp[k, s]
            for c in range(3):
                out_b[s, c, k : k + 1, :] = row(c, idx)
        return carry

    lax.fori_loop(0, NB, fill_brick, 0)
    for s in range(NB):
        out_b[s, 3] = jnp.broadcast_to(rs[:, s : s + 1].astype(f32), (NS, NV))

    def fill_face(i, carry):
        for side in range(2):
            for k in range(8):
                idx = fp[side, i * 8 + k]
                for c in range(3):
                    out_f[side, c, pl.ds(i * 8 + k, 1), :] = row(c, idx)
        return carry

    lax.fori_loop(0, NF // 8, fill_face, 0)
    greeted(barrier, me_t)
    ask_b.start()
    ask_f.start()

    got_b[me_b, 0:3] = jnp.full((3, NS, NV), FAR, f32)
    got_b[me_b, 3] = jnp.zeros((NS, NV), f32)
    ret_b[me_b] = jnp.zeros((3, NS, NV), f32)

    @pl.when(me_t == 0)
    def _():
        got_f[0] = jnp.full((3, NF, NV), FAR, f32)
        ret_f[0] = jnp.zeros((3, NF, NV), f32)

    @pl.when(me_t == 3)
    def _():
        got_f[1] = jnp.full((3, NF, NV), FAR, f32)
        ret_f[1] = jnp.zeros((3, NF, NV), f32)

    def border(i, carry):
        for k in range(8):
            idx = pick[0, i * 8 + k]
            at = pl.ds(i * 8 + k, 1)
            for c in range(3):
                brd[c, at, :] = verts[c, pl.ds(idx, 1), :]
            brd[3, at, :] = stiff[pl.ds(idx, 1), :]
        return carry

    lax.fori_loop(0, NV // 8, border, 0)
    groups = Groups(xg, vg, sg, lx, lc, rx, rc, eb)

    def pushing(u, p, idx):
        for c in range(3):
            vg[u, c, p : p + 1, :] = verts[c, pl.ds(idx, 1), :]
        sg[u, p : p + 1, :] = stiff[pl.ds(idx, 1), :]

    def load_local(u, g):
        for p in range(8):
            a = loc[0, g * 8 + p]
            for c in range(3):
                xg[u, c, p : p + 1, :] = verts[c, pl.ds(a, 1), :]
            pushing(u, p, loc[1, g * 8 + p])

    def put_local(g, push, re):
        for c in range(3):
            push_l[c, rows8(g), :] = push[c]
            react[c, rows8(g), :] = re[c]

    groups.run(0, FIRST, load_local, put_local)

    ask_b.wait()
    ask_f.wait()
    table = jnp.concatenate([brd[c] for c in range(4)], 1)
    t1 = table.astype(bf16)
    r = table - t1.astype(f32)
    t2 = r.astype(bf16)
    t3 = (r - t2.astype(f32)).astype(bf16)
    parts = jnp.concatenate([t1, t2, t3], 0)
    lane = lax.broadcasted_iota(i32, (NV, NV), 1).astype(f32)
    for h in range(NBS // NV):
        want = jnp.concatenate([got_b[h * 16 + s, 3] for s in range(16)], 0)
        for s in range(16):
            meta[h * 16 + s] = got_b[h * 16 + s, 3]
        hot = jnp.where(want == lane, 1.0, 0.0).astype(bf16)
        v = jnp.dot(jnp.concatenate([hot] * 3, 1), parts, preferred_element_type=f32)
        for c in range(4):
            gv[c, h * NV : (h + 1) * NV, :] = v[:, c * NV : (c + 1) * NV]

    def load_brick(u, g):
        for c in range(3):
            xg[u, c] = got_b[g, c]
            vg[u, c] = gv[c, rows8(g), :]
        sg[u] = gv[3, rows8(g), :]

    def put_brick(g, push, re):
        for c in range(3):
            back_b[g, c] = push[c]
            react[c, rows8(g, NL), :] = re[c]

    groups.run(0, NB, load_brick, put_brick)
    give_b.start()

    half = NF // 8

    def load_face(u, g):
        side = g // half
        k = lax.rem(g, half)
        for c in range(3):
            xg[u, c] = got_f[side, c, rows8(k), :]
        for p in range(8):
            pushing(u, p, fpick[side, k * 8 + p])

    def put_face(g, push, re):
        side = g // half
        k = lax.rem(g, half)
        for c in range(3):
            back_f[side, c, rows8(k), :] = push[c]
            react[c, rows8(g, NL + NBS), :] = re[c]

    groups.run(0, 2 * half, load_face, put_face)
    give_f.start()
    groups.run(FIRST, NL // 8 - FIRST, load_local, put_local)
    give_b.wait()
    give_f.wait()


def pairs(rp, fp, loc, pick, fpick, rs, verts, stiff):
    sds = jax.ShapeDtypeStruct
    return pl.pallas_call(
        pair_kernel,
        name="pairs",
        out_shape=(
            sds((3, NL, NV), f32),
            sds((3, NL + NBS + 2 * NF, NV), f32),
            sds((NB, 3, NS, NV), f32),
            sds((2, 3, NF, NV), f32),
            sds((NB, NS, NV), f32),
        ),
        in_specs=[sm] * 5 + [vm] * 3,
        out_specs=(vm,) * 5,
        scratch_shapes=[
            pltpu.VMEM((NB, 4, NS, NV), f32),
            pltpu.VMEM((2, 3, NF, NV), f32),
            pltpu.VMEM((NB, 4, NS, NV), f32),
            pltpu.VMEM((2, 3, NF, NV), f32),
            pltpu.VMEM((NB, 3, NS, NV), f32),
            pltpu.VMEM((2, 3, NF, NV), f32),
            pltpu.VMEM((4, NV, NV), f32),
            pltpu.VMEM((4, NBS, NV), f32),
            pltpu.VMEM((U, 3, 8, NV), f32),
            pltpu.VMEM((U, 3, 8, NV), f32),
            pltpu.VMEM((U, 8, NV), f32),
            *[pltpu.VMEM((U, 64, NV), f32)] * 4,
            pltpu.VMEM((U, 4, 4, NV, NV), bf16),
            pltpu.SemaphoreType.DMA((4, NB)),
            pltpu.SemaphoreType.DMA((4, 2)),
        ],
        compiler_params=pltpu.CompilerParams(
            collective_id=0, has_side_effects=True, vmem_limit_bytes=48 << 20
        ),
    )(rp, fp, loc, pick, fpick, rs, verts, stiff)


def merge_kernel(rp, fp, loc, pick, fpick, push_l, react, ret_b, ret_f, meta, out, *acc):
    me_t = lax.axis_index("slab")
    p1, p2, r1, r2, brd = acc[0:3], acc[3:6], acc[6:9], acc[9:12], acc[12]
    zero = jnp.zeros((64, NV), f32)

    def clear(i, carry):
        for ref in acc[0:12]:
            ref[pl.ds(pl.multiple_of(i * 64, 64), 64), :] = zero
        return carry

    lax.fori_loop(0, NP // 64, clear, 0)

    lane = lax.broadcasted_iota(i32, (NV, NV), 1).astype(f32)
    hots = []
    for h in range(NBS // NV):
        want = jnp.concatenate([meta[h * 16 + s] for s in range(16)], 0)
        hots.append(jnp.where(want == lane, 1.0, 0.0).astype(bf16))
    hot = jnp.concatenate(hots, 0)
    got = jnp.concatenate([react[c, NL : NL + NBS, :] for c in range(3)], 1)
    g1 = got.astype(bf16)
    g2 = got - g1.astype(f32)
    g3 = g2 - g2.astype(bf16).astype(f32)
    parts = jnp.concatenate([g1, g2.astype(bf16), g3.astype(bf16)], 0)
    total = lax.dot_general(
        jnp.concatenate([hot] * 3, 0), parts, D0, preferred_element_type=f32
    )
    for c in range(3):
        brd[c] = total[:, c * NV : (c + 1) * NV]

    def add(refs, idx, values):
        at = pl.ds(idx, 1)
        for c in range(3):
            refs[c][at, :] += values[c]

    def one(i, carry):
        for h in range(2):
            j = i + h * NV
            at = pl.ds(j, 1)
            add(p1, loc[0, j], [push_l[c, at, :] for c in range(3)])
            add(r1, loc[1, j], [react[c, at, :] for c in range(3)])
            s = j // NS
            k = lax.rem(j, NS)
            idx = rp[k, s]
            some = [jnp.where(idx >= 0, ret_b[s, c, pl.ds(k, 1), :], 0.0) for c in range(3)]
            add(p2, jnp.maximum(idx, 0), some)
            if h == 0:
                add(r2, pick[0, i], [brd[c, pl.ds(i, 1), :] for c in range(3)])
            else:
                side = i // NF
                k = lax.rem(i, NF)
                at = pl.ds(NL + NBS + i, 1)
                add(r2, fpick[side, k], [react[c, at, :] for c in range(3)])
                idx = fp[side, k]
                idx = jnp.where(jnp.where(side == 0, me_t > 0, me_t < 3), idx, -1)
                some = [jnp.where(idx >= 0, ret_f[side, c, pl.ds(k, 1), :], 0.0) for c in range(3)]
                add(p2, jnp.maximum(idx, 0), some)
        return carry

    lax.fori_loop(0, NV, one, 0)

    def spread(i, carry):
        at = pl.ds(pl.multiple_of(i * 64, 64), 64)
        for c in range(3):
            r = r1[c][at, :] + r2[c][at, :]
            s = r + pltpu.roll(r, 1, 1) + pltpu.roll(r, 2, 1)
            out[c, at, :] = p1[c][at, :] + p2[c][at, :] + s * (1.0 / 3.0)
        return carry

    lax.fori_loop(0, NP // 64, spread, 0)


def merge(rp, fp, loc, pick, fpick, push_l, react, ret_b, ret_f, meta):
    return pl.pallas_call(
        merge_kernel,
        name="merge",
        out_shape=jax.ShapeDtypeStruct((3, NP, NV), f32),
        in_specs=[sm] * 5 + [vm] * 5,
        out_specs=vm,
        scratch_shapes=[pltpu.VMEM((NP, NV), f32)] * 12 + [pltpu.VMEM((3, NV, NV), f32)],
        compiler_params=pltpu.CompilerParams(vmem_limit_bytes=48 << 20),
    )(rp, fp, loc, pick, fpick, push_l, react, ret_b, ret_f, meta)


def body(verts, stiffness, local_pairs, border_pick, recv_src, recv_pair, face_pick, face_pair):
    rp = recv_pair[0].T
    lists = (rp, face_pair[0], local_pairs[0], border_pick, face_pick[0])
    made = pairs(*lists, recv_src[0].T, verts.transpose(1, 0, 2), stiffness)
    return merge(*lists, *made).transpose(1, 0, 2)


def solution(mesh):
    both = ("slab", "brick")
    placed = (
        P(both, None, None),
        P(both, None),
        P(both, None, None),
        P(both, None),
        P(both, None, None),
        P(both, None, None),
        P(both, None, None),
        P(both, None, None),
    )
    return jax.shard_map(
        body, mesh=mesh, in_specs=placed, out_specs=P(both, None, None), check_vma=False
    )
```

time: 620 us -> 56.5 us (0.09)
  matrix products: 230 us -> 0 us
  local copies, waits for them, and re-layouts: 169 us -> 6.51 us
  other arithmetic: 137 us -> 0 us
  waiting for transfers between devices: 51.9 us -> 0 us
  Pallas kernels: 0 us -> 49.6 us
  between operations: 14.5 us -> 0.02 us
  starting transfers between devices: 10.5 us -> 0 us
    dot_general x120 -> x0, matrix products: 230 us -> none  [the longest x40 96 us: tile_forces(): jnp.einsum('pci,pcj->pij', own_points, far_centres, precision=highest)]
    scatter-add x8 -> x0, other arithmetic: 117 us -> none  [the longest x2 47.8 us: remote(): return (pushed.at[clipped].add(push_far), react_far)]
    gather x77 -> x0, local copies, waits for them, and re-layouts: 117 us -> none  [the longest x24 52.7 us: far_tiles(): return tile_forces(verts[target_idx], centroids(packed_rows[:, :3]), weight)]
    unnamed x3 -> x0, waiting for transfers between devices: 51.9 us -> none
    pallas_call x0 -> x2, Pallas kernels: none -> 49.6 us  [the longest x1 39.5 us: pairs(): pl.pallas_call(pair_kernel, name='pairs', out_shape=(sds((3, NL, NV), f32...]
    squeeze x17 -> x0, local copies, waits for them, and re-layouts: 12.3 us -> none  [the longest x16 12.2 us: blocked(): results = lax.map(func, shaped)]
    all_gather x1 -> x0, local copies, waits for them, and re-layouts: 11.8 us -> none  [body(): lax.all_gather(pack_rows(border_pick[0]), 'brick', axis=0, tiled=True)]
    slice x54 -> x0, local copies, waits for them, and re-layouts: 11.1 us -> none  [the longest x25 4.48 us: centroids(): jnp.roll(points, -2, axis=-1)]
  transfers between devices with their start and end apart: 6 -> 0, of which waited for: 1 -> 0; matrix products, arithmetic and copies ran while one was open for 41% -> 0% of each run, Pallas kernels for 0% -> 0%
where the time goes in v2:
time: 56.5 us; the launch traced here: 56.2 us
  Pallas kernels  49.6 us (88%)
  local copies, waits for them, and re-layouts  6.51 us (12%)
    pallas_call x1, Pallas kernels, pairs(): pl.pallas_call(pair_kernel, name='pairs', out_shape=(sds((3, NL, NV), f32...  39.5 us
    pallas_call x1, Pallas kernels, merge(): pl.pallas_call(merge_kernel, name='merge', out_shape=jax.ShapeDtypeStruct...  10.1 us
    unnamed x16, local copies, waits for them, and re-layouts  6.51 us

profile of v2, /device:TPU:1, one launch (start us, length us, event | category | flops | bytes accessed | tf_op | source)
XLA Modules:
  0.0 56.2 jit_solution(3689927101624735752)
XLA Ops:
  0.0 0.0 copy-start
  0.0 1.4 %copy-done = f32[1024,3,128]{2,0,1:T(8,128)S(1)} copy-done((f32[1024,3,128]{2,0,1:T(8,128)S(1)}, f32[1024,3,128]{2,0,1:T(8,128)}, u32[]{:S(2)}) %copy-start) | copy-done | bytes 1572888
  1.4 0.0 copy-start.1
  1.4 1.0 %copy-done.1 = f32[1024,128]{1,0:T(8,128)S(1)} copy-done((f32[1024,128]{1,0:T(8,128)S(1)}, f32[1024,128]{1,0:T(8,128)}, u32[]{:S(2)}) %copy-start.1) | copy-done | bytes 524312
  2.5 0.0 copy-start.2
  2.5 0.7 %copy-done.2 = s32[1,32,8]{1,2,0:T(8,128)S(1)} copy-done((s32[1,32,8]{1,2,0:T(8,128)S(1)}, s32[1,32,8]{1,2,0:T(8,128)}, u32[]{:S(2)}) %copy-start.2) | copy-done | bytes 1048
  3.1 0.0 copy-start.3
  3.1 0.7 %copy-done.3 = s32[1,2,256]{2,1,0:T(2,128)S(1)} copy-done((s32[1,2,256]{2,1,0:T(2,128)S(1)}, s32[1,2,256]{2,1,0:T(2,128)}, u32[]{:S(2)}) %copy-start.3) | copy-done | bytes 2072
  3.8 0.0 copy-start.4
  3.8 0.7 %copy-done.4 = s32[1,32,8]{1,2,0:T(8,128)S(1)} copy-done((s32[1,32,8]{1,2,0:T(8,128)S(1)}, s32[1,32,8]{1,2,0:T(8,128)}, u32[]{:S(2)}) %copy-start.4) | copy-done | bytes 1048
  4.5 0.0 copy-start.5
  4.5 0.7 %copy-done.5 = s32[1,2,64]{2,1,0:T(2,128)S(1)} copy-done((s32[1,2,64]{2,1,0:T(2,128)S(1)}, s32[1,2,64]{2,1,0:T(2,128)}, u32[]{:S(2)}) %copy-start.5) | copy-done | bytes 536
  5.2 0.0 copy-start.6
  5.2 0.7 %copy-done.6 = s32[1,2,64]{2,1,0:T(2,128)S(1)} copy-done((s32[1,2,64]{2,1,0:T(2,128)S(1)}, s32[1,2,64]{2,1,0:T(2,128)}, u32[]{:S(2)}) %copy-start.6) | copy-done | bytes 536
  5.9 0.0 copy-start.7
  5.9 0.7 %copy-done.7 = s32[1,128]{1,0:T(1,128)S(1)} copy-done((s32[1,128]{1,0:T(1,128)S(1)}, s32[1,128]{1,0:T(1,128)}, u32[]{:S(2)}) %copy-start.7) | copy-done | bytes 536
  6.5 39.5 %pairs.1 = (f32[3,256,128]{2,1,0:T(8,128)S(1)}, f32[3,640,128]{2,1,0:T(8,128)S(1)}, f32[32,3,8,128]{3,2,1,0:T(8,128)S(1)}, f32[2,3,64,128]{3,2,1,0:T(8,128)S(1)}, f32[32,8,128]{2,1,0:T(8,128)S(1)}) custom-call(s32[8,32]{1,0:T(8,128)S(1)} %bitcast.12, s32[2,64]{1,0:T(2,128)S(1)} %bitcast.17, s32[2,256]{1,0:T(2,128)S(1)} %bitcast.14, s32[1,128]{1,0:T(1,128)S(1)} %copy-done.7, ...), custom_call_target="tpu_custom_call" | custom-call | tf_op jit(solution)/shard_map/pairs/pallas_call | solution.py:386
  46.0 10.1 %merge.1 = f32[3,1024,128]{2,1,0:T(8,128)} custom-call(s32[8,32]{1,0:T(8,128)S(1)} %bitcast.13, s32[2,64]{1,0:T(2,128)S(1)} %bitcast.18, s32[2,256]{1,0:T(2,128)S(1)} %bitcast.15, s32[1,128]{1,0:T(1,128)S(1)} %copy-done.7, s32[2,64]{1,0:T(2,128)S(1)} %bitcast.20, f32[3,256,128]{2,1,0:T(8,128)S(1)} %get-tuple-element.10.push_l, ...), custom_call_target="tpu_custom_call" | custom-call | tf_op jit(solution)/shard_map/merge/pallas_call | solution.py:493
Async XLA Ops:
  0.0 1.4 %copy-start = (f32[1024,3,128]{2,0,1:T(8,128)S(1)}, f32[1024,3,128]{2,0,1:T(8,128)}, u32[]{:S(2)}) copy-start(f32[1024,3,128]{2,0,1:T(8,128)} %param.8) | copy-start | bytes 4718596
  1.4 1.0 %copy-start.1 = (f32[1024,128]{1,0:T(8,128)S(1)}, f32[1024,128]{1,0:T(8,128)}, u32[]{:S(2)}) copy-start(f32[1024,128]{1,0:T(8,128)} %stiff.1) | copy-start | bytes 1572868
  2.5 0.7 %copy-start.2 = (s32[1,32,8]{1,2,0:T(8,128)S(1)}, s32[1,32,8]{1,2,0:T(8,128)}, u32[]{:S(2)}) copy-start(s32[1,32,8]{1,2,0:T(8,128)} %param.13) | copy-start | bytes 3076
  3.1 0.7 %copy-start.3 = (s32[1,2,256]{2,1,0:T(2,128)S(1)}, s32[1,2,256]{2,1,0:T(2,128)}, u32[]{:S(2)}) copy-start(s32[1,2,256]{2,1,0:T(2,128)} %param.10) | copy-start | bytes 6148
  3.8 0.7 %copy-start.4 = (s32[1,32,8]{1,2,0:T(8,128)S(1)}, s32[1,32,8]{1,2,0:T(8,128)}, u32[]{:S(2)}) copy-start(s32[1,32,8]{1,2,0:T(8,128)} %param.12) | copy-start | bytes 3076
  4.5 0.7 %copy-start.5 = (s32[1,2,64]{2,1,0:T(2,128)S(1)}, s32[1,2,64]{2,1,0:T(2,128)}, u32[]{:S(2)}) copy-start(s32[1,2,64]{2,1,0:T(2,128)} %param.15) | copy-start | bytes 1540
  5.2 0.7 %copy-start.6 = (s32[1,2,64]{2,1,0:T(2,128)S(1)}, s32[1,2,64]{2,1,0:T(2,128)}, u32[]{:S(2)}) copy-start(s32[1,2,64]{2,1,0:T(2,128)} %param.14) | copy-start | bytes 1540
  5.9 0.7 %copy-start.7 = (s32[1,128]{1,0:T(1,128)S(1)}, s32[1,128]{1,0:T(1,128)}, u32[]{:S(2)}) copy-start(s32[1,128]{1,0:T(1,128)} %pick.3) | copy-start | bytes 1540

commit v3 on v2

--- a/solution.py
+++ b/solution.py
@@ -23,12 +23,14 @@
 SQ = math.sqrt(math.log2(math.e))
 FAR = 1.0e4
 U = 4
+CHUNKS = 4
 LAG = 4
 DN = (((1,), (1,)), ((), ()))
 D0 = (((0,), (0,)), ((), ()))
 
 vm = pl.BlockSpec(memory_space=pltpu.VMEM)
-sm = pl.BlockSpec(memory_space=pltpu.SMEM)
+hbm = pl.BlockSpec(memory_space=pltpu.HBM)
+LISTS = ((NS, NB), (2, NF), (2, NL), (1, NV), (2, NF))
 
 
 def greet(me_t, me_b):
@@ -235,19 +237,30 @@
             second(j, first + count - U + j // 4)
 
 
-def rows8(g, base=0):
-    return pl.ds(pl.multiple_of(base + g * 8, 8), 8)
+def rows8(g):
+    return pl.ds(pl.multiple_of(g * 8, 8), 8)
 
 
 def pair_kernel(
-    rp, fp, loc, pick, fpick, rs, verts, stiff,
-    push_l, react, ret_b, ret_f, meta,
-    got_b, got_f, out_b, out_f, back_b, back_f, brd, gv,
-    xg, vg, sg, lx, lc, rx, rc, eb, sems, fsems,
+    *refs,
 ):
+    ins, refs = refs[:8], refs[8:]
+    outs, refs = refs[:5], refs[5:]
+    ret_b, ret_f, *refs = refs
+    here, refs = refs[:8], refs[8:]
+    rp, fp, loc, pick, fpick, rs, verts, stiff = here
+    made, refs = refs[:5], refs[5:]
+    push_l, react_l, react_b, react_f, meta = made
+    got_b, got_f, out_b, out_f, back_b, back_f, brd, gv, *work, sems, fsems, isems, osems = refs
+    xg, vg, sg = work[:3]
     me_t = lax.axis_index("slab")
     me_b = lax.axis_index("brick")
+    moves = [pltpu.make_async_copy(a, b, isems.at[k]) for k, (a, b) in enumerate(zip(ins, here))]
+    for move in moves:
+        move.start()
     barrier = greet(me_t, me_b)
+    for move in moves:
+        move.wait()
     ask_b = Brick(out_b, got_b, sems.at[0], sems.at[1], me_t, me_b)
     ask_f = Face(out_f, got_f, fsems.at[0], fsems.at[1], me_t, me_b)
     give_b = Brick(back_b, ret_b, sems.at[2], sems.at[3], me_t, me_b)
@@ -282,17 +295,14 @@
 
     got_b[me_b, 0:3] = jnp.full((3, NS, NV), FAR, f32)
     got_b[me_b, 3] = jnp.zeros((NS, NV), f32)
-    ret_b[me_b] = jnp.zeros((3, NS, NV), f32)
 
     @pl.when(me_t == 0)
     def _():
         got_f[0] = jnp.full((3, NF, NV), FAR, f32)
-        ret_f[0] = jnp.zeros((3, NF, NV), f32)
 
     @pl.when(me_t == 3)
     def _():
         got_f[1] = jnp.full((3, NF, NV), FAR, f32)
-        ret_f[1] = jnp.zeros((3, NF, NV), f32)
 
     def border(i, carry):
         for k in range(8):
@@ -304,7 +314,7 @@
         return carry
 
     lax.fori_loop(0, NV // 8, border, 0)
-    groups = Groups(xg, vg, sg, lx, lc, rx, rc, eb)
+    groups = Groups(*work)
 
     def pushing(u, p, idx):
         for c in range(3):
@@ -321,9 +331,20 @@
     def put_local(g, push, re):
         for c in range(3):
             push_l[c, rows8(g), :] = push[c]
-            react[c, rows8(g), :] = re[c]
+            react_l[c, rows8(g), :] = re[c]
+
+    def out_copy(k, rows=None, slot=None):
+        a, b = made[k], outs[k]
+        if rows is not None:
+            a, b = a.at[:, rows, :], b.at[:, rows, :]
+        return pltpu.make_async_copy(a, b, osems.at[k if slot is None else slot])
 
     groups.run(0, FIRST, load_local, put_local)
+    early = pl.ds(0, 8 * FIRST)
+    late = pl.ds(8 * FIRST, NL - 8 * FIRST)
+    copies = [out_copy(0, early), out_copy(1, early)]
+    for copy in copies:
+        copy.start()
 
     ask_b.wait()
     ask_f.wait()
@@ -352,10 +373,14 @@
     def put_brick(g, push, re):
         for c in range(3):
             back_b[g, c] = push[c]
-            react[c, rows8(g, NL), :] = re[c]
+            react_b[c, rows8(g), :] = re[c]
 
     groups.run(0, NB, load_brick, put_brick)
     give_b.start()
+    copies += [out_copy(2), out_copy(4)]
+    copies.append(pltpu.make_async_copy(back_b.at[me_b], ret_b.at[me_b], osems.at[7]))
+    for copy in copies[2:]:
+        copy.start()
 
     half = NF // 8
 
@@ -372,13 +397,37 @@
         k = lax.rem(g, half)
         for c in range(3):
             back_f[side, c, rows8(k), :] = push[c]
-            react[c, rows8(g, NL + NBS), :] = re[c]
+            react_f[c, rows8(g), :] = re[c]
 
     groups.run(0, 2 * half, load_face, put_face)
     give_f.start()
+    copies.append(out_copy(3))
+    copies[-1].start()
+    ends = [pltpu.make_async_copy(back_f.at[k], ret_f.at[k], osems.at[8]) for k in range(2)]
+    for side in range(2):
+
+        @pl.when(jnp.logical_not(give_f.there(side)))
+        def _(side=side):
+            ends[side].start()
+
     groups.run(FIRST, NL // 8 - FIRST, load_local, put_local)
+    copies += [out_copy(0, late, 5), out_copy(1, late, 6)]
+    for copy in copies[-2:]:
+        copy.start()
     give_b.wait()
     give_f.wait()
+    for side in range(2):
+
+        @pl.when(jnp.logical_not(give_f.there(side)))
+        def _(side=side):
+            ends[side].wait()
+
+    for copy in copies:
+        copy.wait()
+
+
+MADE = ((3, NL, NV), (3, NL, NV), (3, NBS, NV), (3, 2 * NF, NV), (NB, NS, NV))
+BACK = ((NB, 3, NS, NV), (2, 3, NF, NV))
 
 
 def pairs(rp, fp, loc, pick, fpick, rs, verts, stiff):
@@ -386,16 +435,15 @@
     return pl.pallas_call(
         pair_kernel,
         name="pairs",
-        out_shape=(
-            sds((3, NL, NV), f32),
-            sds((3, NL + NBS + 2 * NF, NV), f32),
-            sds((NB, 3, NS, NV), f32),
-            sds((2, 3, NF, NV), f32),
-            sds((NB, NS, NV), f32),
-        ),
-        in_specs=[sm] * 5 + [vm] * 3,
-        out_specs=(vm,) * 5,
+        out_shape=tuple(sds(shape, f32) for shape in MADE + BACK),
+        in_specs=[hbm] * 8,
+        out_specs=(hbm,) * 7,
         scratch_shapes=[
+            *[pltpu.SMEM(shape, i32) for shape in LISTS],
+            pltpu.VMEM((NS, NB), i32),
+            pltpu.VMEM((3, NP, NV), f32),
+            pltpu.VMEM((NP, NV), f32),
+            *[pltpu.VMEM(shape, f32) for shape in MADE],
             pltpu.VMEM((NB, 4, NS, NV), f32),
             pltpu.VMEM((2, 3, NF, NV), f32),
             pltpu.VMEM((NB, 4, NS, NV), f32),
@@ -411,94 +459,99 @@
             pltpu.VMEM((U, 4, 4, NV, NV), bf16),
             pltpu.SemaphoreType.DMA((4, NB)),
             pltpu.SemaphoreType.DMA((4, 2)),
+            pltpu.SemaphoreType.DMA((8,)),
+            pltpu.SemaphoreType.DMA((9,)),
         ],
-        compiler_params=pltpu.CompilerParams(
-            collective_id=0, has_side_effects=True, vmem_limit_bytes=48 << 20
-        ),
+        compiler_params=pltpu.CompilerParams(collective_id=0, has_side_effects=True),
     )(rp, fp, loc, pick, fpick, rs, verts, stiff)
 
 
-def merge_kernel(rp, fp, loc, pick, fpick, push_l, react, ret_b, ret_f, meta, out, *acc):
-    me_t = lax.axis_index("slab")
-    p1, p2, r1, r2, brd = acc[0:3], acc[3:6], acc[6:9], acc[9:12], acc[12]
-    zero = jnp.zeros((64, NV), f32)
-
-    def clear(i, carry):
-        for ref in acc[0:12]:
-            ref[pl.ds(pl.multiple_of(i * 64, 64), 64), :] = zero
-        return carry
-
-    lax.fori_loop(0, NP // 64, clear, 0)
+def flat(a):
+    lane = lax.broadcasted_iota(i32, (NB, NBS), 1)
+    wide = (lane // NS == lax.broadcasted_iota(i32, (NB, NBS), 0)).astype(f32).astype(bf16)
+    high, low = split(a.astype(f32))
+    row = jnp.dot(high.astype(bf16), wide, preferred_element_type=f32)
+    row = row + jnp.dot(low.astype(bf16), wide, preferred_element_type=f32)
+    own = lax.broadcasted_iota(i32, (NS, NBS), 0) == lax.broadcasted_iota(i32, (NS, NBS), 1) % NS
+    return jnp.sum(jnp.where(own, row, 0.0), axis=0, keepdims=True)
+
+
+def two(x):
+    high, low = split(x)
+    return high.astype(bf16), low.astype(bf16)
+
+
+def side_by_side(a):
+    return jnp.concatenate([a[0:1], a[1:2]], 1).astype(f32)
+
+
+def merge_kernel(*refs):
+    n_in = 5 + len(MADE) + len(BACK)
+    ins, out, here, refs = refs[:n_in], refs[n_in], refs[n_in + 1 : 2 * n_in + 1], refs[2 * n_in + 1 :]
+    rp, fp, loc, pick, fpick, push_l, react_l, react_b, react_f, meta, ret_b, ret_f = here
+    made, isems, osems = refs
+    moves = [pltpu.make_async_copy(a, b, isems.at[k]) for k, (a, b) in enumerate(zip(ins, here))]
+    for move in moves:
+        move.start()
+    for move in moves:
+        move.wait()
+    cat = jnp.concatenate
+
+    def lanes(ref):
+        return cat([ref[c] for c in range(3)], 1)
 
     lane = lax.broadcasted_iota(i32, (NV, NV), 1).astype(f32)
     hots = []
     for h in range(NBS // NV):
-        want = jnp.concatenate([meta[h * 16 + s] for s in range(16)], 0)
+        want = cat([meta[h * 16 + s] for s in range(16)], 0)
         hots.append(jnp.where(want == lane, 1.0, 0.0).astype(bf16))
-    hot = jnp.concatenate(hots, 0)
-    got = jnp.concatenate([react[c, NL : NL + NBS, :] for c in range(3)], 1)
-    g1 = got.astype(bf16)
-    g2 = got - g1.astype(f32)
-    g3 = g2 - g2.astype(bf16).astype(f32)
-    parts = jnp.concatenate([g1, g2.astype(bf16), g3.astype(bf16)], 0)
-    total = lax.dot_general(
-        jnp.concatenate([hot] * 3, 0), parts, D0, preferred_element_type=f32
-    )
-    for c in range(3):
-        brd[c] = total[:, c * NV : (c + 1) * NV]
-
-    def add(refs, idx, values):
-        at = pl.ds(idx, 1)
-        for c in range(3):
-            refs[c][at, :] += values[c]
-
-    def one(i, carry):
-        for h in range(2):
-            j = i + h * NV
-            at = pl.ds(j, 1)
-            add(p1, loc[0, j], [push_l[c, at, :] for c in range(3)])
-            add(r1, loc[1, j], [react[c, at, :] for c in range(3)])
-            s = j // NS
-            k = lax.rem(j, NS)
-            idx = rp[k, s]
-            some = [jnp.where(idx >= 0, ret_b[s, c, pl.ds(k, 1), :], 0.0) for c in range(3)]
-            add(p2, jnp.maximum(idx, 0), some)
-            if h == 0:
-                add(r2, pick[0, i], [brd[c, pl.ds(i, 1), :] for c in range(3)])
-            else:
-                side = i // NF
-                k = lax.rem(i, NF)
-                at = pl.ds(NL + NBS + i, 1)
-                add(r2, fpick[side, k], [react[c, at, :] for c in range(3)])
-                idx = fp[side, k]
-                idx = jnp.where(jnp.where(side == 0, me_t > 0, me_t < 3), idx, -1)
-                some = [jnp.where(idx >= 0, ret_f[side, c, pl.ds(k, 1), :], 0.0) for c in range(3)]
-                add(p2, jnp.maximum(idx, 0), some)
-        return carry
-
-    lax.fori_loop(0, NV, one, 0)
-
-    def spread(i, carry):
-        at = pl.ds(pl.multiple_of(i * 64, 64), 64)
-        for c in range(3):
-            r = r1[c][at, :] + r2[c][at, :]
+    hot = cat(hots, 0)
+    border = lax.dot_general(cat([hot] * 2, 0), cat(two(lanes(react_b)), 0), D0, preferred_element_type=f32)
+
+    back_b = cat([cat([ret_b[s, c] for s in range(NB)], 0) for c in range(3)], 1)
+    back_f = cat([cat([ret_f[k, c] for k in range(2)], 0) for c in range(3)], 1)
+    push = cat(two(cat([lanes(push_l), back_b, back_f], 0)), 0)
+    react = cat(two(cat([lanes(react_l), border, lanes(react_f)], 0)), 0)
+    pushed = cat([loc[0:1].astype(f32), flat(rp[...]), side_by_side(fp[...])], 1)
+    pushing = cat([loc[1:2].astype(f32), pick[...].astype(f32), side_by_side(fpick[...])], 1)
+
+    size = NP // CHUNKS
+    copies = []
+    for n in range(CHUNKS):
+
+        def scatter(idx, values):
+            row = lax.broadcasted_iota(i32, (size, idx.shape[1]), 0).astype(f32) + float(n * size)
+            one = jnp.where(row == idx, 1.0, 0.0).astype(bf16)
+            return jnp.dot(cat([one, one], 1), values, preferred_element_type=f32)
+
+        p = scatter(pushed, push)
+        q = scatter(pushing, react)
+        rows = pl.ds(n * size, size)
+        for c in range(3):
+            r = q[:, c * NV : (c + 1) * NV]
             s = r + pltpu.roll(r, 1, 1) + pltpu.roll(r, 2, 1)
-            out[c, at, :] = p1[c][at, :] + p2[c][at, :] + s * (1.0 / 3.0)
-        return carry
-
-    lax.fori_loop(0, NP // 64, spread, 0)
-
-
-def merge(rp, fp, loc, pick, fpick, push_l, react, ret_b, ret_f, meta):
+            made[c, rows, :] = p[:, c * NV : (c + 1) * NV] + s * (1.0 / 3.0)
+        copies.append(pltpu.make_async_copy(made.at[:, rows, :], out.at[:, rows, :], osems.at[n]))
+        copies[-1].start()
+    for copy in copies:
+        copy.wait()
+
+
+def merge(*args):
     return pl.pallas_call(
         merge_kernel,
         name="merge",
         out_shape=jax.ShapeDtypeStruct((3, NP, NV), f32),
-        in_specs=[sm] * 5 + [vm] * 5,
-        out_specs=vm,
-        scratch_shapes=[pltpu.VMEM((NP, NV), f32)] * 12 + [pltpu.VMEM((3, NV, NV), f32)],
-        compiler_params=pltpu.CompilerParams(vmem_limit_bytes=48 << 20),
-    )(rp, fp, loc, pick, fpick, push_l, react, ret_b, ret_f, meta)
+        in_specs=[hbm] * len(args),
+        out_specs=hbm,
+        scratch_shapes=[
+            *[pltpu.VMEM(shape, i32) for shape in LISTS],
+            *[pltpu.VMEM(shape, f32) for shape in MADE + BACK],
+            pltpu.VMEM((3, NP, NV), f32),
+            pltpu.SemaphoreType.DMA((len(args),)),
+            pltpu.SemaphoreType.DMA((CHUNKS,)),
+        ],
+    )(*args)
 
 
 def body(verts, stiffness, local_pairs, border_pick, recv_src, recv_pair, face_pick, face_pair):

time: 56.5 us -> 44.9 us (0.79)
  local copies, waits for them, and re-layouts: 6.51 us -> 0 us
  Pallas kernels: 49.6 us -> 44.8 us
    unnamed x16 -> x0, local copies, waits for them, and re-layouts: 6.51 us -> none
    pallas_call x1, Pallas kernels: 10.1 us -> 5.49 us  [merge(): pl.pallas_call(merge_kernel, name='merge', out_shape=jax.ShapeDtypeStruct...]
where the time goes in v3:
time: 44.9 us; the launch traced here: 44.8 us
  Pallas kernels  44.8 us (100%)
    pallas_call x1, Pallas kernels, pairs(): pl.pallas_call(pair_kernel, name='pairs', out_shape=tuple((sds(shape, f32...  39.3 us
    pallas_call x1, Pallas kernels, merge(): pl.pallas_call(merge_kernel, name='merge', out_shape=jax.ShapeDtypeStruct...  5.49 us

profile of v3, /device:TPU:1, one launch (start us, length us, event | category | flops | bytes accessed | tf_op | source)
XLA Modules:
  0.0 44.8 jit_solution(5760487078626524391)
XLA Ops:
  0.0 39.3 %pairs.1 = (f32[3,256,128]{2,1,0:T(8,128)}, f32[3,256,128]{2,1,0:T(8,128)}, f32[3,256,128]{2,1,0:T(8,128)}, f32[3,128,128]{2,1,0:T(8,128)}, f32[32,8,128]{2,1,0:...) custom-call(s32[8,32]{1,0:T(8,128)} %bitcast.12, s32[2,64]{1,0:T(2,128)} %bitcast.17, s32[2,256]{1,0:T(2,128)} %bitcast.14, ...), custom_call_target="tpu_custom_call" | custom-call | tf_op jit(solution)/shard_map/pairs/pallas_call | solution.py:435
  39.3 5.5 %merge.1 = f32[3,1024,128]{2,1,0:T(8,128)} custom-call(s32[8,32]{1,0:T(8,128)} %bitcast.13, s32[2,64]{1,0:T(2,128)} %bitcast.18, s32[2,256]{1,0:T(2,128)} %bitcast.15, s32[1,128]{1,0:T(1,128)} %refs_3_.3, s32[2,64]{1,0:T(2,128)} %bitcast.20, f32[3,256,128]{2,1,0:T(8,128)} %get-tuple-element.12.refs_5_, f32[3,256,128]{2,1,0:T(8,128)} %get-tuple-element.13.refs_6_, ...), custom_call_target="tpu_custom_call" | custom-call | tf_op jit(solution)/shard_map/merge/pallas_call | solution.py:541

commit v4 on v3

--- a/solution.py
+++ b/solution.py
@@ -19,7 +19,7 @@
 NF = 64
 NBS = NB * NS
 NL = 256
-FIRST = 20
+FIRST = 16
 SQ = math.sqrt(math.log2(math.e))
 FAR = 1.0e4
 U = 4
@@ -199,7 +199,7 @@
     def __init__(self, xg, vg, sg, lx, lc, rx, rc, eb):
         self.r = (xg, vg, sg, lx, lc, rx, rc, eb)
 
-    def run(self, first, count, load, put):
+    def run(self, first, count, load, put, after=None):
         xg, vg, sg, lx, lc, rx, rc, eb = self.r
         n = U * 4
 
@@ -230,11 +230,16 @@
                 eb[u, t, 1] = low[:, :NV]
                 eb[u, t, 2] = high[:, NV:]
                 eb[u, t, 3] = low[:, NV:]
+            if after is not None:
+                for u in range(U):
+                    after(base + u - 1)
             return carry
 
         lax.fori_loop(0, count // U, step, 0)
         for j in range(n - LAG, n):
             second(j, first + count - U + j // 4)
+        if after is not None:
+            after(first + count - 1)
 
 
 def rows8(g):
@@ -269,30 +274,8 @@
     def row(c, idx):
         return jnp.where(idx >= 0, verts[c, pl.ds(jnp.maximum(idx, 0), 1), :], FAR)
 
-    def fill_brick(s, carry):
-        for k in range(NS):
-            idx = rp[k, s]
-            for c in range(3):
-                out_b[s, c, k : k + 1, :] = row(c, idx)
-        return carry
-
-    lax.fori_loop(0, NB, fill_brick, 0)
     for s in range(NB):
         out_b[s, 3] = jnp.broadcast_to(rs[:, s : s + 1].astype(f32), (NS, NV))
-
-    def fill_face(i, carry):
-        for side in range(2):
-            for k in range(8):
-                idx = fp[side, i * 8 + k]
-                for c in range(3):
-                    out_f[side, c, pl.ds(i * 8 + k, 1), :] = row(c, idx)
-        return carry
-
-    lax.fori_loop(0, NF // 8, fill_face, 0)
-    greeted(barrier, me_t)
-    ask_b.start()
-    ask_f.start()
-
     got_b[me_b, 0:3] = jnp.full((3, NS, NV), FAR, f32)
     got_b[me_b, 3] = jnp.zeros((NS, NV), f32)
 
@@ -304,17 +287,8 @@
     def _():
         got_f[1] = jnp.full((3, NF, NV), FAR, f32)
 
-    def border(i, carry):
-        for k in range(8):
-            idx = pick[0, i * 8 + k]
-            at = pl.ds(i * 8 + k, 1)
-            for c in range(3):
-                brd[c, at, :] = verts[c, pl.ds(idx, 1), :]
-            brd[3, at, :] = stiff[pl.ds(idx, 1), :]
-        return carry
-
-    lax.fori_loop(0, NV // 8, border, 0)
     groups = Groups(*work)
+    half = NF // 8
 
     def pushing(u, p, idx):
         for c in range(3):
@@ -328,26 +302,75 @@
                 xg[u, c, p : p + 1, :] = verts[c, pl.ds(a, 1), :]
             pushing(u, p, loc[1, g * 8 + p])
 
+    def load_first(u, g):
+        load_local(u, g)
+        for h in range(2):
+            s = 2 * g + h
+            for k in range(NS):
+                for c in range(3):
+                    out_b[s, c, k : k + 1, :] = row(c, rp[k, s])
+        side = g // half
+        for k in range(8):
+            j = lax.rem(g, half) * 8 + k
+            for c in range(3):
+                out_f[side, c, pl.ds(j, 1), :] = row(c, fp[side, j])
+
+    def load_second(u, g):
+        load_local(u, g)
+        for k in range(8):
+            j = (g - FIRST) * 8 + k
+            idx = pick[0, j]
+            for c in range(3):
+                brd[c, pl.ds(j, 1), :] = verts[c, pl.ds(idx, 1), :]
+            brd[3, pl.ds(j, 1), :] = stiff[pl.ds(idx, 1), :]
+
     def put_local(g, push, re):
         for c in range(3):
             push_l[c, rows8(g), :] = push[c]
             react_l[c, rows8(g), :] = re[c]
 
-    def out_copy(k, rows=None, slot=None):
-        a, b = made[k], outs[k]
-        if rows is not None:
-            a, b = a.at[:, rows, :], b.at[:, rows, :]
-        return pltpu.make_async_copy(a, b, osems.at[k if slot is None else slot])
-
-    groups.run(0, FIRST, load_local, put_local)
-    early = pl.ds(0, 8 * FIRST)
-    late = pl.ds(8 * FIRST, NL - 8 * FIRST)
-    copies = [out_copy(0, early), out_copy(1, early)]
-    for copy in copies:
-        copy.start()
+    groups.run(0, FIRST, load_first, put_local)
+    greeted(barrier, me_t)
+    ask_f.start()
+    ask_b.start()
+    groups.run(FIRST, NL // 8 - FIRST, load_second, put_local)
+
+    copies = []
+
+    def give_out(k):
+        copies.append(pltpu.make_async_copy(made[k], outs[k], osems.at[k]))
+        copies[-1].start()
+
+    give_out(0)
+    give_out(1)
+
+    def load_face(u, g):
+        side = g // half
+        k = lax.rem(g, half)
+        for c in range(3):
+            xg[u, c] = got_f[side, c, rows8(k), :]
+        for p in range(8):
+            pushing(u, p, fpick[side, k * 8 + p])
+
+    def put_face(g, push, re):
+        side = g // half
+        k = lax.rem(g, half)
+        for c in range(3):
+            back_f[side, c, rows8(k), :] = push[c]
+            react_f[c, rows8(g), :] = re[c]
+
+    ask_f.wait()
+    groups.run(0, 2 * half, load_face, put_face)
+    give_f.start()
+    give_out(3)
+    ends = [pltpu.make_async_copy(back_f.at[k], ret_f.at[k], fsems.at[4, k]) for k in range(2)]
+    for side in range(2):
+
+        @pl.when(jnp.logical_not(give_f.there(side)))
+        def _(side=side):
+            ends[side].start()
 
     ask_b.wait()
-    ask_f.wait()
     table = jnp.concatenate([brd[c] for c in range(4)], 1)
     t1 = table.astype(bf16)
     r = table - t1.astype(f32)
@@ -364,56 +387,30 @@
         for c in range(4):
             gv[c, h * NV : (h + 1) * NV, :] = v[:, c * NV : (c + 1) * NV]
 
-    def load_brick(u, g):
-        for c in range(3):
-            xg[u, c] = got_b[g, c]
-            vg[u, c] = gv[c, rows8(g), :]
-        sg[u] = gv[3, rows8(g), :]
-
-    def put_brick(g, push, re):
-        for c in range(3):
-            back_b[g, c] = push[c]
-            react_b[c, rows8(g), :] = re[c]
-
-    groups.run(0, NB, load_brick, put_brick)
-    give_b.start()
-    copies += [out_copy(2), out_copy(4)]
-    copies.append(pltpu.make_async_copy(back_b.at[me_b], ret_b.at[me_b], osems.at[7]))
-    for copy in copies[2:]:
-        copy.start()
-
-    half = NF // 8
-
-    def load_face(u, g):
-        side = g // half
-        k = lax.rem(g, half)
-        for c in range(3):
-            xg[u, c] = got_f[side, c, rows8(k), :]
-        for p in range(8):
-            pushing(u, p, fpick[side, k * 8 + p])
-
-    def put_face(g, push, re):
-        side = g // half
-        k = lax.rem(g, half)
-        for c in range(3):
-            back_f[side, c, rows8(k), :] = push[c]
-            react_f[c, rows8(g), :] = re[c]
-
-    groups.run(0, 2 * half, load_face, put_face)
-    give_f.start()
-    copies.append(out_copy(3))
-    copies[-1].start()
-    ends = [pltpu.make_async_copy(back_f.at[k], ret_f.at[k], osems.at[8]) for k in range(2)]
-    for side in range(2):
-
-        @pl.when(jnp.logical_not(give_f.there(side)))
-        def _(side=side):
-            ends[side].start()
-
-    groups.run(FIRST, NL // 8 - FIRST, load_local, put_local)
-    copies += [out_copy(0, late, 5), out_copy(1, late, 6)]
-    for copy in copies[-2:]:
-        copy.start()
+    give_out(4)
+
+    def load_brick(u, o):
+        s = lax.rem(me_b + o, NB)
+        for c in range(3):
+            xg[u, c] = got_b[s, c]
+            vg[u, c] = gv[c, rows8(s), :]
+        sg[u] = gv[3, rows8(s), :]
+
+    def put_brick(o, push, re):
+        s = lax.rem(me_b + o, NB)
+        for c in range(3):
+            back_b[s, c] = push[c]
+            react_b[c, rows8(s), :] = re[c]
+
+    def send_back(o):
+        @pl.when(o >= 1)
+        def _():
+            give_b.copy(o).start()
+
+    groups.run(0, NB, load_brick, put_brick, send_back)
+    give_out(2)
+    own = pltpu.make_async_copy(back_b.at[me_b], ret_b.at[me_b], osems.at[5])
+    own.start()
     give_b.wait()
     give_f.wait()
     for side in range(2):
@@ -422,6 +419,7 @@
         def _(side=side):
             ends[side].wait()
 
+    own.wait()
     for copy in copies:
         copy.wait()
 
@@ -458,9 +456,9 @@
             *[pltpu.VMEM((U, 64, NV), f32)] * 4,
             pltpu.VMEM((U, 4, 4, NV, NV), bf16),
             pltpu.SemaphoreType.DMA((4, NB)),
-            pltpu.SemaphoreType.DMA((4, 2)),
+            pltpu.SemaphoreType.DMA((5, 2)),
             pltpu.SemaphoreType.DMA((8,)),
-            pltpu.SemaphoreType.DMA((9,)),
+            pltpu.SemaphoreType.DMA((6,)),
         ],
         compiler_params=pltpu.CompilerParams(collective_id=0, has_side_effects=True),
     )(rp, fp, loc, pick, fpick, rs, verts, stiff)

time: 44.9 us -> 45.4 us (1.011)
  no operation moved by 1% of the time
where the time goes in v4:
time: 45.4 us; the launch traced here: 45.2 us
  Pallas kernels  45.2 us (100%)
    pallas_call x1, Pallas kernels, pairs(): pl.pallas_call(pair_kernel, name='pairs', out_shape=tuple((sds(shape, f32...  39.7 us
    pallas_call x1, Pallas kernels, merge(): pl.pallas_call(merge_kernel, name='merge', out_shape=jax.ShapeDtypeStruct...  5.49 us

profile of v4, /device:TPU:1, one launch (start us, length us, event | category | flops | bytes accessed | tf_op | source)
XLA Modules:
  0.0 45.2 jit_solution(16348195690140056325)
XLA Ops:
  0.0 39.7 %pairs.1 = (f32[3,256,128]{2,1,0:T(8,128)}, f32[3,256,128]{2,1,0:T(8,128)}, f32[3,256,128]{2,1,0:T(8,128)}, f32[3,128,128]{2,1,0:T(8,128)}, f32[32,8,128]{2,1,0:...) custom-call(s32[8,32]{1,0:T(8,128)} %bitcast.12, s32[2,64]{1,0:T(2,128)} %bitcast.17, s32[2,256]{1,0:T(2,128)} %bitcast.14, ...), custom_call_target="tpu_custom_call" | custom-call | tf_op jit(solution)/shard_map/pairs/pallas_call | solution.py:433
  39.7 5.5 %merge.1 = f32[3,1024,128]{2,1,0:T(8,128)} custom-call(s32[8,32]{1,0:T(8,128)} %bitcast.13, s32[2,64]{1,0:T(2,128)} %bitcast.18, s32[2,256]{1,0:T(2,128)} %bitcast.15, s32[1,128]{1,0:T(1,128)} %refs_3_.3, s32[2,64]{1,0:T(2,128)} %bitcast.20, f32[3,256,128]{2,1,0:T(8,128)} %get-tuple-element.12.refs_5_, f32[3,256,128]{2,1,0:T(8,128)} %get-tuple-element.13.refs_6_, ...), custom_call_target="tpu_custom_call" | custom-call | tf_op jit(solution)/shard_map/merge/pallas_call | solution.py:539

commit v5 on v4

--- a/solution.py
+++ b/solution.py
@@ -20,9 +20,10 @@
 NBS = NB * NS
 NL = 256
 FIRST = 16
+SECOND = 8
 SQ = math.sqrt(math.log2(math.e))
 FAR = 1.0e4
-U = 4
+U = 16
 CHUNKS = 4
 LAG = 4
 DN = (((1,), (1,)), ((), ()))
@@ -199,47 +200,55 @@
     def __init__(self, xg, vg, sg, lx, lc, rx, rc, eb):
         self.r = (xg, vg, sg, lx, lc, rx, rc, eb)
 
-    def run(self, first, count, load, put, after=None):
+    def second(self, i, g, put):
         xg, vg, sg, lx, lc, rx, rc, eb = self.r
-        n = U * 4
-
-        def second(i, g):
+        u, t = divmod(i, 4)
+        e = [eb[u, t, k] for k in range(4)]
+        sums(t, e, lx.at[u], lc.at[u], rx.at[u], rc.at[u])
+        if t == 3:
+            xs = [xg[u, c] for c in range(3)]
+            cs = [vg[u, c] for c in range(3)]
+            put(g, *forces(xs, cs, rx.at[u], rc.at[u]))
+
+    def phase(self, base, count, load, put, before=None):
+        xg, vg, sg, lx, lc, rx, rc, eb = self.r
+        for i in range(count * 4):
             u, t = divmod(i, 4)
-            e = [eb[u, t, k] for k in range(4)]
-            sums(t, e, lx.at[u], lc.at[u], rx.at[u], rc.at[u])
-            if t == 3:
+            if t == 0:
+                load(u, base + u)
                 xs = [xg[u, c] for c in range(3)]
-                cs = [vg[u, c] for c in range(3)]
-                put(g, *forces(xs, cs, rx.at[u], rc.at[u]))
-
+                cs, at, b = prepare(xs, [vg[u, c] for c in range(3)], sg[u], lx.at[u], lc.at[u])
+                for c in range(3):
+                    vg[u, c] = cs[c]
+            j = i - LAG
+            if j >= 0:
+                self.second(j, base + j // 4, put)
+            elif before is not None:
+                n, last, put_last = before
+                self.second(n * 4 + j, last, put_last)
+            high, low = energies(at, b, t)
+            eb[u, t, 0] = high[:, :NV]
+            eb[u, t, 1] = low[:, :NV]
+            eb[u, t, 2] = high[:, NV:]
+            eb[u, t, 3] = low[:, NV:]
+        return count, base + count - 1, put
+
+    def flush(self, before):
+        n, last, put = before
+        for j in range(n * 4 - LAG, n * 4):
+            self.second(j, last, put)
+
+    def loop(self, total, count, load, put, after):
         def step(s, carry):
-            base = first + s * U
-            for i in range(n):
-                u, t = divmod(i, 4)
-                if t == 0:
-                    load(u, base + u)
-                    xs = [xg[u, c] for c in range(3)]
-                    cs, at, b = prepare(xs, [vg[u, c] for c in range(3)], sg[u], lx.at[u], lc.at[u])
-                    for c in range(3):
-                        vg[u, c] = cs[c]
-                j = i - LAG
-                ju = (j % n) // 4
-                second(j % n, base + ju if j >= 0 else jnp.maximum(base + ju - U, first))
-                high, low = energies(at, b, t)
-                eb[u, t, 0] = high[:, :NV]
-                eb[u, t, 1] = low[:, :NV]
-                eb[u, t, 2] = high[:, NV:]
-                eb[u, t, 3] = low[:, NV:]
-            if after is not None:
-                for u in range(U):
-                    after(base + u - 1)
+            base = s * count
+            self.phase(base, count, load, put, (count, jnp.maximum(base - 1, 0), put))
+            for u in range(count):
+                after(base + u - 1)
             return carry
 
-        lax.fori_loop(0, count // U, step, 0)
-        for j in range(n - LAG, n):
-            second(j, first + count - U + j // 4)
-        if after is not None:
-            after(first + count - 1)
+        lax.fori_loop(0, total // count, step, 0)
+        self.flush((count, total - 1, put))
+        after(total - 1)
 
 
 def rows8(g):
@@ -317,8 +326,8 @@
 
     def load_second(u, g):
         load_local(u, g)
-        for k in range(8):
-            j = (g - FIRST) * 8 + k
+        for k in range(16):
+            j = (g - FIRST) * 16 + k
             idx = pick[0, j]
             for c in range(3):
                 brd[c, pl.ds(j, 1), :] = verts[c, pl.ds(idx, 1), :]
@@ -329,21 +338,17 @@
             push_l[c, rows8(g), :] = push[c]
             react_l[c, rows8(g), :] = re[c]
 
-    groups.run(0, FIRST, load_first, put_local)
+    tail = groups.phase(0, FIRST, load_first, put_local)
     greeted(barrier, me_t)
     ask_f.start()
     ask_b.start()
-    groups.run(FIRST, NL // 8 - FIRST, load_second, put_local)
-
+    tail = groups.phase(FIRST, SECOND, load_second, put_local, tail)
     copies = []
 
     def give_out(k):
         copies.append(pltpu.make_async_copy(made[k], outs[k], osems.at[k]))
         copies[-1].start()
 
-    give_out(0)
-    give_out(1)
-
     def load_face(u, g):
         side = g // half
         k = lax.rem(g, half)
@@ -360,7 +365,7 @@
             react_f[c, rows8(g), :] = re[c]
 
     ask_f.wait()
-    groups.run(0, 2 * half, load_face, put_face)
+    groups.flush(groups.phase(0, 2 * half, load_face, put_face, tail))
     give_f.start()
     give_out(3)
     ends = [pltpu.make_async_copy(back_f.at[k], ret_f.at[k], fsems.at[4, k]) for k in range(2)]
@@ -407,10 +412,14 @@
         def _():
             give_b.copy(o).start()
 
-    groups.run(0, NB, load_brick, put_brick, send_back)
+    groups.loop(NB, U, load_brick, put_brick, send_back)
     give_out(2)
     own = pltpu.make_async_copy(back_b.at[me_b], ret_b.at[me_b], osems.at[5])
     own.start()
+    late = FIRST + SECOND
+    groups.flush(groups.phase(late, NL // 8 - late, load_local, put_local))
+    give_out(0)
+    give_out(1)
     give_b.wait()
     give_f.wait()
     for side in range(2):

time: 45.4 us -> 41.1 us (0.905)
  Pallas kernels: 45.2 us -> 40.8 us
    pallas_call x1, Pallas kernels: 39.7 us -> 35.3 us  [pairs(): pl.pallas_call(pair_kernel, name='pairs', out_shape=tuple((sds(shape, f32...]
where the time goes in v5:
time: 41.1 us; the launch traced here: 41 us
  Pallas kernels  40.8 us (99%)
    pallas_call x1, Pallas kernels, pairs(): pl.pallas_call(pair_kernel, name='pairs', out_shape=tuple((sds(shape, f32...  35.3 us
    pallas_call x1, Pallas kernels, merge(): pl.pallas_call(merge_kernel, name='merge', out_shape=jax.ShapeDtypeStruct...  5.49 us

profile of v5, /device:TPU:1, one launch (start us, length us, event | category | flops | bytes accessed | tf_op | source)
XLA Modules:
  0.0 41.0 jit_solution(838054860678265500)
XLA Ops:
  0.0 35.3 %pairs.1 = (f32[3,256,128]{2,1,0:T(8,128)}, f32[3,256,128]{2,1,0:T(8,128)}, f32[3,256,128]{2,1,0:T(8,128)}, f32[3,128,128]{2,1,0:T(8,128)}, f32[32,8,128]{2,1,0:...) custom-call(s32[8,32]{1,0:T(8,128)} %bitcast.12, s32[2,64]{1,0:T(2,128)} %bitcast.17, s32[2,256]{1,0:T(2,128)} %bitcast.14, ...), custom_call_target="tpu_custom_call" | custom-call | tf_op jit(solution)/shard_map/pairs/pallas_call | solution.py:442
  35.3 5.5 %merge.1 = f32[3,1024,128]{2,1,0:T(8,128)} custom-call(s32[8,32]{1,0:T(8,128)} %bitcast.13, s32[2,64]{1,0:T(2,128)} %bitcast.18, s32[2,256]{1,0:T(2,128)} %bitcast.15, s32[1,128]{1,0:T(1,128)} %refs_3_.3, s32[2,64]{1,0:T(2,128)} %bitcast.20, f32[3,256,128]{2,1,0:T(8,128)} %get-tuple-element.12.refs_5_, f32[3,256,128]{2,1,0:T(8,128)} %get-tuple-element.13.refs_6_, ...), custom_call_target="tpu_custom_call" | custom-call | tf_op jit(solution)/shard_map/merge/pallas_call | solution.py:548

commit v6 on v5

--- a/solution.py
+++ b/solution.py
@@ -138,7 +138,7 @@
     return pltpu.roll(v, NV - k, 1)
 
 
-def prepare(xs, vs, stiff, lx, lc):
+def prepare(xs, vs, stiff, lx, lc, ab):
     one = jnp.ones((8, NV), f32)
     zero = jnp.zeros((8, NV), f32)
     cs = [(v + ahead(v, 1) + ahead(v, 2)) * (1.0 / 3.0) for v in vs]
@@ -152,19 +152,27 @@
     n2, n3 = split(r)
     m1, r = split(m)
     m2, m3 = split(r)
-    a = jnp.concatenate([*x1, *x1, *x2, n1, n2, n3, one, one, one, zero], 0).astype(bf16)
-    b = jnp.concatenate([*c1, *c2, *c1, one, one, one, m1, m2, m3, zero], 0).astype(bf16)
+    for k, r in enumerate([*x1, *x1, *x2, n1, n2, n3, one, one, one, zero]):
+        ab[0, 8 * k : 8 * k + 8, :] = r
+    for k, r in enumerate([*c1, *c2, *c1, one, one, one, m1, m2, m3, zero]):
+        ab[1, 8 * k : 8 * k + 8, :] = r
     for ref, rows in ((lx, [*x1, *x2, one, zero]), (lc, [*c1, *c2, one, zero])):
         for k, r in enumerate(rows):
             ref[pl.ds(k, 8, stride=8), :] = r
-    return cs, a.T, b
-
-
-def energies(at, b, t):
-    sub = lax.broadcasted_iota(i32, (NV, NV), 0) % 8
-    zero = jnp.zeros_like(b)
-    two = jnp.concatenate([jnp.where(sub == 2 * t + k, b, zero) for k in range(2)], 1)
-    e = jnp.exp2(jnp.dot(at, two, preferred_element_type=f32))
+    return cs
+
+
+def energies(ab, t):
+    def get(side, p):
+        return ab[side, pl.ds(p, 16, stride=8), :].astype(bf16)
+
+    cat = jnp.concatenate
+    a = cat([get(0, 2 * t), get(0, 2 * t + 1)], 0).T
+    b0 = get(1, 2 * t)
+    b1 = get(1, 2 * t + 1)
+    zero = jnp.zeros_like(b0)
+    b = cat([cat([b0, zero], 1), cat([zero, b1], 1)], 0)
+    e = jnp.exp2(jnp.dot(a, b, preferred_element_type=f32))
     high = e.astype(bf16)
     return high, (e - high.astype(f32)).astype(bf16)
 
@@ -197,11 +205,11 @@
 
 
 class Groups:
-    def __init__(self, xg, vg, sg, lx, lc, rx, rc, eb):
-        self.r = (xg, vg, sg, lx, lc, rx, rc, eb)
+    def __init__(self, xg, vg, sg, lx, lc, rx, rc, eb, ab):
+        self.r = (xg, vg, sg, lx, lc, rx, rc, eb, ab)
 
     def second(self, i, g, put):
-        xg, vg, sg, lx, lc, rx, rc, eb = self.r
+        xg, vg, sg, lx, lc, rx, rc, eb, ab = self.r
         u, t = divmod(i, 4)
         e = [eb[u, t, k] for k in range(4)]
         sums(t, e, lx.at[u], lc.at[u], rx.at[u], rc.at[u])
@@ -211,13 +219,14 @@
             put(g, *forces(xs, cs, rx.at[u], rc.at[u]))
 
     def phase(self, base, count, load, put, before=None):
-        xg, vg, sg, lx, lc, rx, rc, eb = self.r
+        xg, vg, sg, lx, lc, rx, rc, eb, ab = self.r
         for i in range(count * 4):
             u, t = divmod(i, 4)
             if t == 0:
                 load(u, base + u)
                 xs = [xg[u, c] for c in range(3)]
-                cs, at, b = prepare(xs, [vg[u, c] for c in range(3)], sg[u], lx.at[u], lc.at[u])
+                vs = [vg[u, c] for c in range(3)]
+                cs = prepare(xs, vs, sg[u], lx.at[u], lc.at[u], ab.at[u])
                 for c in range(3):
                     vg[u, c] = cs[c]
             j = i - LAG
@@ -226,7 +235,7 @@
             elif before is not None:
                 n, last, put_last = before
                 self.second(n * 4 + j, last, put_last)
-            high, low = energies(at, b, t)
+            high, low = energies(ab.at[u], t)
             eb[u, t, 0] = high[:, :NV]
             eb[u, t, 1] = low[:, :NV]
             eb[u, t, 2] = high[:, NV:]
@@ -464,6 +473,7 @@
             pltpu.VMEM((U, 8, NV), f32),
             *[pltpu.VMEM((U, 64, NV), f32)] * 4,
             pltpu.VMEM((U, 4, 4, NV, NV), bf16),
+            pltpu.VMEM((U, 2, NV, NV), f32),
             pltpu.SemaphoreType.DMA((4, NB)),
             pltpu.SemaphoreType.DMA((5, 2)),
             pltpu.SemaphoreType.DMA((8,)),
@@ -498,10 +508,11 @@
     rp, fp, loc, pick, fpick, push_l, react_l, react_b, react_f, meta, ret_b, ret_f = here
     made, isems, osems = refs
     moves = [pltpu.make_async_copy(a, b, isems.at[k]) for k, (a, b) in enumerate(zip(ins, here))]
-    for move in moves:
-        move.start()
-    for move in moves:
-        move.wait()
+    order = [9, 7, 0, 1, 2, 3, 4, 5, 6, 8, 10, 11]
+    for k in order:
+        moves[k].start()
+    for k in order[:2]:
+        moves[k].wait()
     cat = jnp.concatenate
 
     def lanes(ref):
@@ -514,13 +525,17 @@
         hots.append(jnp.where(want == lane, 1.0, 0.0).astype(bf16))
     hot = cat(hots, 0)
     border = lax.dot_general(cat([hot] * 2, 0), cat(two(lanes(react_b)), 0), D0, preferred_element_type=f32)
+    for k in order[2:7]:
+        moves[k].wait()
+    pushed = cat([loc[0:1].astype(f32), flat(rp[...]), side_by_side(fp[...])], 1)
+    pushing = cat([loc[1:2].astype(f32), pick[...].astype(f32), side_by_side(fpick[...])], 1)
+    for k in order[7:]:
+        moves[k].wait()
 
     back_b = cat([cat([ret_b[s, c] for s in range(NB)], 0) for c in range(3)], 1)
     back_f = cat([cat([ret_f[k, c] for k in range(2)], 0) for c in range(3)], 1)
     push = cat(two(cat([lanes(push_l), back_b, back_f], 0)), 0)
     react = cat(two(cat([lanes(react_l), border, lanes(react_f)], 0)), 0)
-    pushed = cat([loc[0:1].astype(f32), flat(rp[...]), side_by_side(fp[...])], 1)
-    pushing = cat([loc[1:2].astype(f32), pick[...].astype(f32), side_by_side(fpick[...])], 1)
 
     size = NP // CHUNKS
     copies = []

time: 41.1 us -> 39.8 us (0.968)
  Pallas kernels: 40.8 us -> 39.5 us
    pallas_call x1, Pallas kernels: 35.3 us -> 34.2 us  [pairs(): pl.pallas_call(pair_kernel, name='pairs', out_shape=tuple((sds(shape, f32...]
where the time goes in v6:
time: 39.8 us; the launch traced here: 39.7 us
  Pallas kernels  39.5 us (99%)
    pallas_call x1, Pallas kernels, pairs(): pl.pallas_call(pair_kernel, name='pairs', out_shape=tuple((sds(shape, f32...  34.2 us
    pallas_call x1, Pallas kernels, merge(): pl.pallas_call(merge_kernel, name='merge', out_shape=jax.ShapeDtypeStruct...  5.32 us

profile of v6, /device:TPU:1, one launch (start us, length us, event | category | flops | bytes accessed | tf_op | source)
XLA Modules:
  0.0 39.7 jit_solution(17020087275778244943)
XLA Ops:
  0.0 34.2 %pairs.1 = (f32[3,256,128]{2,1,0:T(8,128)}, f32[3,256,128]{2,1,0:T(8,128)}, f32[3,256,128]{2,1,0:T(8,128)}, f32[3,128,128]{2,1,0:T(8,128)}, f32[32,8,128]{2,1,0:...) custom-call(s32[8,32]{1,0:T(8,128)} %bitcast.12, s32[2,64]{1,0:T(2,128)} %bitcast.17, s32[2,256]{1,0:T(2,128)} %bitcast.14, ...), custom_call_target="tpu_custom_call" | custom-call | tf_op jit(solution)/shard_map/pairs/pallas_call | solution.py:451
  34.2 5.3 %merge.1 = f32[3,1024,128]{2,1,0:T(8,128)} custom-call(s32[8,32]{1,0:T(8,128)} %bitcast.13, s32[2,64]{1,0:T(2,128)} %bitcast.18, s32[2,256]{1,0:T(2,128)} %bitcast.15, s32[1,128]{1,0:T(1,128)} %refs_3_.3, s32[2,64]{1,0:T(2,128)} %bitcast.20, f32[3,256,128]{2,1,0:T(8,128)} %get-tuple-element.12.refs_5_, f32[3,256,128]{2,1,0:T(8,128)} %get-tuple-element.13.refs_6_, ...), custom_call_target="tpu_custom_call" | custom-call | tf_op jit(solution)/shard_map/merge/pallas_call | solution.py:563

commit v7 on v6

--- a/solution.py
+++ b/solution.py
@@ -20,7 +20,7 @@
 NBS = NB * NS
 NL = 256
 FIRST = 16
-SECOND = 8
+SECOND = 4
 SQ = math.sqrt(math.log2(math.e))
 FAR = 1.0e4
 U = 16
@@ -65,15 +65,14 @@
     def __init__(self, src, dst, s_sem, r_sem, me_t, me_b):
         self.a = (src, dst, s_sem, r_sem, me_t, me_b)
 
-    def copy(self, o, arrival=False):
+    def copy(self, o):
         src, dst, s_sem, r_sem, me_t, me_b = self.a
         peer = lax.rem(me_b + o, NB)
-        at = peer if arrival else me_b
         return pltpu.make_async_remote_copy(
             src_ref=src.at[peer],
-            dst_ref=dst.at[at],
-            send_sem=s_sem.at[peer],
-            recv_sem=r_sem.at[at],
+            dst_ref=dst.at[me_b],
+            send_sem=s_sem,
+            recv_sem=r_sem,
             device_id=(me_t, peer),
             device_id_type=MESH,
         )
@@ -85,13 +84,23 @@
 
         lax.fori_loop(1, NB, one, 0)
 
-    def wait(self):
-        def one(o, c):
-            self.copy(o, True).wait_recv()
-            self.copy(o).wait_send()
-            return c
-
-        lax.fori_loop(1, NB, one, 0)
+    def all(self):
+        src, dst, s_sem, r_sem, me_t, me_b = self.a
+        rest = pl.ds(0, NB - 1)
+        return pltpu.make_async_remote_copy(
+            src_ref=src.at[rest],
+            dst_ref=dst.at[rest],
+            send_sem=s_sem,
+            recv_sem=r_sem,
+            device_id=(me_t, lax.rem(me_b + 1, NB)),
+            device_id_type=MESH,
+        )
+
+    def wait_recv(self):
+        self.all().wait_recv()
+
+    def wait_send(self):
+        self.all().wait_send()
 
 
 class Face:
@@ -333,15 +342,6 @@
             for c in range(3):
                 out_f[side, c, pl.ds(j, 1), :] = row(c, fp[side, j])
 
-    def load_second(u, g):
-        load_local(u, g)
-        for k in range(16):
-            j = (g - FIRST) * 16 + k
-            idx = pick[0, j]
-            for c in range(3):
-                brd[c, pl.ds(j, 1), :] = verts[c, pl.ds(idx, 1), :]
-            brd[3, pl.ds(j, 1), :] = stiff[pl.ds(idx, 1), :]
-
     def put_local(g, push, re):
         for c in range(3):
             push_l[c, rows8(g), :] = push[c]
@@ -351,7 +351,7 @@
     greeted(barrier, me_t)
     ask_f.start()
     ask_b.start()
-    tail = groups.phase(FIRST, SECOND, load_second, put_local, tail)
+    tail = groups.phase(FIRST, SECOND, load_local, put_local, tail)
     copies = []
 
     def give_out(k):
@@ -365,6 +365,11 @@
             xg[u, c] = got_f[side, c, rows8(k), :]
         for p in range(8):
             pushing(u, p, fpick[side, k * 8 + p])
+            j = g * 8 + p
+            idx = pick[0, j]
+            for c in range(3):
+                brd[c, pl.ds(j, 1), :] = verts[c, pl.ds(idx, 1), :]
+            brd[3, pl.ds(j, 1), :] = stiff[pl.ds(idx, 1), :]
 
     def put_face(g, push, re):
         side = g // half
@@ -384,7 +389,7 @@
         def _(side=side):
             ends[side].start()
 
-    ask_b.wait()
+    ask_b.wait_recv()
     table = jnp.concatenate([brd[c] for c in range(4)], 1)
     t1 = table.astype(bf16)
     r = table - t1.astype(f32)
@@ -429,7 +434,9 @@
     groups.flush(groups.phase(late, NL // 8 - late, load_local, put_local))
     give_out(0)
     give_out(1)
-    give_b.wait()
+    ask_b.wait_send()
+    give_b.wait_recv()
+    give_b.wait_send()
     give_f.wait()
     for side in range(2):
 
@@ -474,7 +481,7 @@
             *[pltpu.VMEM((U, 64, NV), f32)] * 4,
             pltpu.VMEM((U, 4, 4, NV, NV), bf16),
             pltpu.VMEM((U, 2, NV, NV), f32),
-            pltpu.SemaphoreType.DMA((4, NB)),
+            pltpu.SemaphoreType.DMA((4,)),
             pltpu.SemaphoreType.DMA((5, 2)),
             pltpu.SemaphoreType.DMA((8,)),
             pltpu.SemaphoreType.DMA((6,)),

time: 39.8 us -> 38.1 us (0.957)
  Pallas kernels: 39.5 us -> 37.7 us
    pallas_call x1, Pallas kernels: 34.2 us -> 32.4 us  [pairs(): pl.pallas_call(pair_kernel, name='pairs', out_shape=tuple((sds(shape, f32...]
where the time goes in v7:
time: 38.1 us; the launch traced here: 37.9 us
  Pallas kernels  37.7 us (99%)
    pallas_call x1, Pallas kernels, pairs(): pl.pallas_call(pair_kernel, name='pairs', out_shape=tuple((sds(shape, f32...  32.4 us
    pallas_call x1, Pallas kernels, merge(): pl.pallas_call(merge_kernel, name='merge', out_shape=jax.ShapeDtypeStruct...  5.32 us

profile of v7, /device:TPU:1, one launch (start us, length us, event | category | flops | bytes accessed | tf_op | source)
XLA Modules:
  0.0 37.9 jit_solution(17809181318344663381)
XLA Ops:
  0.0 32.4 %pairs.1 = (f32[3,256,128]{2,1,0:T(8,128)}, f32[3,256,128]{2,1,0:T(8,128)}, f32[3,256,128]{2,1,0:T(8,128)}, f32[3,128,128]{2,1,0:T(8,128)}, f32[32,8,128]{2,1,0:...) custom-call(s32[8,32]{1,0:T(8,128)} %bitcast.12, s32[2,64]{1,0:T(2,128)} %bitcast.17, s32[2,256]{1,0:T(2,128)} %bitcast.14, ...), custom_call_target="tpu_custom_call" | custom-call | tf_op jit(solution)/shard_map/pairs/pallas_call | solution.py:458
  32.4 5.3 %merge.1 = f32[3,1024,128]{2,1,0:T(8,128)} custom-call(s32[8,32]{1,0:T(8,128)} %bitcast.13, s32[2,64]{1,0:T(2,128)} %bitcast.18, s32[2,256]{1,0:T(2,128)} %bitcast.15, s32[1,128]{1,0:T(1,128)} %refs_3_.3, s32[2,64]{1,0:T(2,128)} %bitcast.20, f32[3,256,128]{2,1,0:T(8,128)} %get-tuple-element.12.refs_5_, f32[3,256,128]{2,1,0:T(8,128)} %get-tuple-element.13.refs_6_, ...), custom_call_target="tpu_custom_call" | custom-call | tf_op jit(solution)/shard_map/merge/pallas_call | solution.py:570

commit v8 on v7

--- a/solution.py
+++ b/solution.py
@@ -287,7 +287,11 @@
     xg, vg, sg = work[:3]
     me_t = lax.axis_index("slab")
     me_b = lax.axis_index("brick")
-    moves = [pltpu.make_async_copy(a, b, isems.at[k]) for k, (a, b) in enumerate(zip(ins, here))]
+    halves = [pl.ds(h * (NP // 2), NP // 2) for h in range(2)]
+    moves = [(ins[6].at[c, h, :], verts.at[c, h, :]) for c in range(3) for h in halves]
+    moves += [(ins[7].at[h, :], stiff.at[h, :]) for h in halves]
+    moves += list(zip(ins[:6], here[:6]))
+    moves = [pltpu.make_async_copy(a, b, isems.at[k]) for k, (a, b) in enumerate(moves)]
     for move in moves:
         move.start()
     barrier = greet(me_t, me_b)
@@ -354,9 +358,16 @@
     tail = groups.phase(FIRST, SECOND, load_local, put_local, tail)
     copies = []
 
-    def give_out(k):
-        copies.append(pltpu.make_async_copy(made[k], outs[k], osems.at[k]))
+    def give_out(k, rows=None, slot=None):
+        a, b = made[k], outs[k]
+        if rows is not None:
+            a, b = a.at[:, rows, :], b.at[:, rows, :]
+        copies.append(pltpu.make_async_copy(a, b, osems.at[k if slot is None else slot]))
         copies[-1].start()
+
+    cut = 8 * (FIRST + SECOND)
+    early = pl.ds(0, cut)
+    rest = pl.ds(cut, NL - cut)
 
     def load_face(u, g):
         side = g // half
@@ -382,6 +393,8 @@
     groups.flush(groups.phase(0, 2 * half, load_face, put_face, tail))
     give_f.start()
     give_out(3)
+    give_out(0, early)
+    give_out(1, early)
     ends = [pltpu.make_async_copy(back_f.at[k], ret_f.at[k], fsems.at[4, k]) for k in range(2)]
     for side in range(2):
 
@@ -432,8 +445,8 @@
     own.start()
     late = FIRST + SECOND
     groups.flush(groups.phase(late, NL // 8 - late, load_local, put_local))
-    give_out(0)
-    give_out(1)
+    give_out(0, rest, 6)
+    give_out(1, rest, 7)
     ask_b.wait_send()
     give_b.wait_recv()
     give_b.wait_send()
@@ -483,8 +496,8 @@
             pltpu.VMEM((U, 2, NV, NV), f32),
             pltpu.SemaphoreType.DMA((4,)),
             pltpu.SemaphoreType.DMA((5, 2)),
+            pltpu.SemaphoreType.DMA((14,)),
             pltpu.SemaphoreType.DMA((8,)),
-            pltpu.SemaphoreType.DMA((6,)),
         ],
         compiler_params=pltpu.CompilerParams(collective_id=0, has_side_effects=True),
     )(rp, fp, loc, pick, fpick, rs, verts, stiff)

time: 38.1 us -> 38.1 us (level)
  no operation moved by 1% of the time
where the time goes in v8:
time: 38.1 us; the launch traced here: 37.9 us
  Pallas kernels  37.8 us (99%)
    pallas_call x1, Pallas kernels, pairs(): pl.pallas_call(pair_kernel, name='pairs', out_shape=tuple((sds(shape, f32...  32.4 us
    pallas_call x1, Pallas kernels, merge(): pl.pallas_call(merge_kernel, name='merge', out_shape=jax.ShapeDtypeStruct...  5.32 us

profile of v8, /device:TPU:1, one launch (start us, length us, event | category | flops | bytes accessed | tf_op | source)
XLA Modules:
  0.0 37.9 jit_solution(12458209797246369980)
XLA Ops:
  0.0 32.4 %pairs.1 = (f32[3,256,128]{2,1,0:T(8,128)}, f32[3,256,128]{2,1,0:T(8,128)}, f32[3,256,128]{2,1,0:T(8,128)}, f32[3,128,128]{2,1,0:T(8,128)}, f32[32,8,128]{2,1,0:...) custom-call(s32[8,32]{1,0:T(8,128)} %bitcast.12, s32[2,64]{1,0:T(2,128)} %bitcast.17, s32[2,256]{1,0:T(2,128)} %bitcast.14, ...), custom_call_target="tpu_custom_call" | custom-call | tf_op jit(solution)/shard_map/pairs/pallas_call | solution.py:471
  32.4 5.3 %merge.1 = f32[3,1024,128]{2,1,0:T(8,128)} custom-call(s32[8,32]{1,0:T(8,128)} %bitcast.13, s32[2,64]{1,0:T(2,128)} %bitcast.18, s32[2,256]{1,0:T(2,128)} %bitcast.15, s32[1,128]{1,0:T(1,128)} %refs_3_.3, s32[2,64]{1,0:T(2,128)} %bitcast.20, f32[3,256,128]{2,1,0:T(8,128)} %get-tuple-element.12.refs_5_, f32[3,256,128]{2,1,0:T(8,128)} %get-tuple-element.13.refs_6_, ...), custom_call_target="tpu_custom_call" | custom-call | tf_op jit(solution)/shard_map/merge/pallas_call | solution.py:583
